TPU v7x, 128 devices: a whole 4x4x4 slice. The times are simulated.
128 devices in a mesh: dp: 2 (over core), ctx: 16 (over z, y), tp: 4 (over x).
Axes of the slice: x: 4, y: 4, z: 4, core: 2. Of those that a mesh axis runs over, the one named last changes fastest.
Arguments:
- query: bfloat16 [8192, 32, 128], P(('dp', 'ctx'), 'tp'), parts along dimension 0, may hold values from -30 to 30
- keys: bfloat16 [8192, 4, 128], P(('dp', 'ctx'), 'tp'), parts along dimension 0, may hold values from -6 to 6
- values: bfloat16 [8192, 4, 128], P(('dp', 'ctx'), 'tp'), parts along dimension 0, may hold values from -6 to 6
- output_gradient: bfloat16 [8192, 32, 128], P(('dp', 'ctx'), 'tp'), parts along dimension 0, may hold values from -6 to 6
- doc_lengths: int32 [16], P('dp'), parts along dimension 0, may hold values from 1 to 2048, 4096 in all
- block_owner: int32 [32, 16], P('dp'), parts along dimension 0, may hold values from 0 to 15, each once within a row
Outputs:
- attended: bfloat16 [8192, 32, 128], P(('dp', 'ctx'), 'tp'), parts along dimension 0
- query_grad: bfloat16 [8192, 32, 128], P(('dp', 'ctx'), 'tp'), parts along dimension 0
- key_grad: bfloat16 [8192, 4, 128], P(('dp', 'ctx'), 'tp'), parts along dimension 0
- value_grad: bfloat16 [8192, 4, 128], P(('dp', 'ctx'), 'tp'), parts along dimension 0
There are 2 independent parts, one for each index of `dp`. A program takes and returns all parts, laid end to end along the dimension named above; each array names one. Nothing has to cross between parts.
Inputs may be any that keep to these rules, and one draw needn't show every extreme that they name: `block_owner`: each row lists the owners of one loader shard's 16 blocks in order and names every owner once. `doc_lengths`: the lengths sum to 4096.
All inputs are finite; a program needn't handle non-finite values.
Results may differ from a plain program's by a relative error of at most 0.039.
Values may be sent and summed in bfloat16 or wider, within the bound.
A program may use at most 64 MiB of HBM per device.

v0:
```python
import jax
import jax.numpy as jnp
from jax import lax
from jax.sharding import PartitionSpec as P

NEG_LARGE = -1e30


def passed_along(array, axis, by):
    size = lax.axis_size(axis)
    return lax.ppermute(array, axis, [(i, (i + by) % size) for i in range(size)])


def document_index(token_positions, doc_lengths):
    doc_ends = jnp.cumsum(doc_lengths)
    return jnp.sum((doc_ends[None, :] <= token_positions[:, None]).astype(jnp.int32), axis=1)


def owner_positions(block_owner, owner_id, local_rows):
    cycle_size = block_owner.shape[0]
    block_rows = local_rows // cycle_size
    slot_ids = jnp.arange(cycle_size, dtype=jnp.int32)
    matches = (block_owner == owner_id).astype(jnp.int32)
    slot_of = jnp.sum(matches * slot_ids[None, :], axis=1)
    starts = slot_ids * local_rows + slot_of * block_rows
    return (starts[:, None] + jnp.arange(block_rows, dtype=jnp.int32)[None, :]).reshape(-1)


def on_device(query, keys, values, output_gradient, doc_lengths, block_owner):
    cycle_size = lax.axis_size("ctx")
    own_index = lax.axis_index("ctx")
    local_rows, heads_here, head_width = query.shape
    groups_here = keys.shape[1]
    heads_per_group = heads_here // groups_here
    block_rows = local_rows // cycle_size
    softmax_scale = head_width ** (-0.5)
    own_targets = lax.dynamic_index_in_dim(block_owner, own_index, 0, keepdims=False)
    slot_ids = jnp.arange(cycle_size, dtype=jnp.int32)
    send_order = jnp.sum(
        (own_targets[:, None] == slot_ids[None, :]).astype(jnp.int32) * slot_ids[:, None], axis=0
    )

    def arrange(source):
        return jnp.take(source.reshape(cycle_size, block_rows, -1), send_order, axis=0)

    loaded_pairs = jnp.stack([keys, values], axis=1)
    received = (
        lax.all_to_all(arrange(query), "ctx", split_axis=0, concat_axis=0, tiled=True),
        lax.all_to_all(arrange(loaded_pairs), "ctx", split_axis=0, concat_axis=0, tiled=True),
        lax.all_to_all(arrange(output_gradient), "ctx", split_axis=0, concat_axis=0, tiled=True),
    )
    query_rows_all = received[0].reshape(local_rows, groups_here, heads_per_group, head_width)
    key_value = received[1].reshape(local_rows, 2, groups_here, head_width)
    output_gradients = received[2].reshape(local_rows, groups_here, heads_per_group, head_width)
    query_pos = owner_positions(block_owner, own_index, local_rows)
    query_doc = document_index(query_pos, doc_lengths)

    def visible(owner_id):
        key_pos = owner_positions(block_owner, owner_id, local_rows)
        key_doc = document_index(key_pos, doc_lengths)
        return (query_doc[:, None] == key_doc[None, :]) & (key_pos[None, :] <= query_pos[:, None])

    def forward_tile(softmax_state, pair_rows, allowed):
        row_max, row_sum, totals = softmax_state
        scores = (
            jnp.einsum(
                "tgrd,ugd->tgru",
                query_rows_all,
                pair_rows[:, 0],
                preferred_element_type=jnp.float32,
            )
            * softmax_scale
        )
        allowed = allowed[:, None, None, :]
        scores = jnp.where(allowed, scores, NEG_LARGE)
        new_max = jnp.maximum(row_max, jnp.max(scores, axis=-1))
        weights = jnp.where(allowed, jnp.exp(scores - new_max[..., None]), 0.0)
        rescale = jnp.exp(row_max - new_max)
        row_sum = row_sum * rescale + jnp.sum(weights, axis=-1)
        totals = totals * rescale[..., None] + jnp.einsum(
            "tgru,ugd->tgrd",
            weights.astype(jnp.bfloat16),
            pair_rows[:, 1],
            preferred_element_type=jnp.float32,
        )
        return (new_max, row_sum, totals)

    stat_shape = (local_rows, groups_here, heads_per_group)
    softmax_state = (
        jnp.full(stat_shape, NEG_LARGE, jnp.float32),
        jnp.zeros(stat_shape, jnp.float32),
        jnp.zeros(query_rows_all.shape, jnp.float32),
    )
    softmax_state = forward_tile(softmax_state, key_value, visible(own_index))

    def forward_turn(turn_index, loop_state):
        moving, partial_state = loop_state
        moving = passed_along(moving, "ctx", 1)
        owner_id = (own_index - turn_index) % cycle_size
        return (moving, forward_tile(partial_state, moving, visible(owner_id)))

    softmax_state = lax.fori_loop(1, cycle_size, forward_turn, (key_value, softmax_state))[1]
    row_max, row_sum, totals = softmax_state
    attended = (totals / row_sum[..., None]).astype(jnp.bfloat16)
    log_sums = row_max + jnp.log(row_sum)
    row_delta_sum = jnp.sum(
        output_gradients.astype(jnp.float32) * attended.astype(jnp.float32), axis=-1
    )

    def backward_tile(pair_rows, allowed):
        scores = (
            jnp.einsum(
                "tgrd,ugd->tgru",
                query_rows_all,
                pair_rows[:, 0],
                preferred_element_type=jnp.float32,
            )
            * softmax_scale
        )
        probs = jnp.where(allowed[:, None, None, :], jnp.exp(scores - log_sums[..., None]), 0.0)
        value_part = jnp.einsum(
            "tgru,tgrd->ugd",
            probs.astype(jnp.bfloat16),
            output_gradients,
            preferred_element_type=jnp.float32,
        )
        products = jnp.einsum(
            "tgrd,ugd->tgru", output_gradients, pair_rows[:, 1], preferred_element_type=jnp.float32
        )
        slopes = (probs * (products - row_delta_sum[..., None])).astype(jnp.bfloat16)
        query_part = (
            jnp.einsum(
                "tgru,ugd->tgrd", slopes, pair_rows[:, 0], preferred_element_type=jnp.float32
            )
            * softmax_scale
        )
        key_part = (
            jnp.einsum("tgru,tgrd->ugd", slopes, query_rows_all, preferred_element_type=jnp.float32)
            * softmax_scale
        )
        return (query_part, jnp.stack([key_part, value_part], axis=1))

    query_grad, pair_grad = backward_tile(key_value, visible(own_index))

    def backward_turn(turn_index, loop_state):
        moving, moving_grad, query_acc = loop_state
        moving = passed_along(moving, "ctx", 1)
        moving_grad = passed_along(moving_grad.astype(jnp.bfloat16), "ctx", 1).astype(
            moving_grad.dtype
        )
        owner_id = (own_index - turn_index) % cycle_size
        query_part, pair_part = backward_tile(moving, visible(owner_id))
        return (moving, moving_grad + pair_part, query_acc + query_part)

    loop_out = lax.fori_loop(1, cycle_size, backward_turn, (key_value, pair_grad, query_grad))
    pair_grad = passed_along(loop_out[1].astype(jnp.bfloat16), "ctx", 1).astype(jnp.float32)
    query_grad = loop_out[2]
    return (
        attended.reshape(local_rows, heads_here, head_width),
        query_grad.astype(jnp.bfloat16).reshape(local_rows, heads_here, head_width),
        pair_grad[:, 0].astype(jnp.bfloat16),
        pair_grad[:, 1].astype(jnp.bfloat16),
    )


def solution(mesh):
    placed = (
        P(("dp", "ctx"), "tp", None),
        P(("dp", "ctx"), "tp", None),
        P(("dp", "ctx"), "tp", None),
        P(("dp", "ctx"), "tp", None),
        P("dp"),
        P("dp", None),
    )
    return jax.shard_map(
        on_device,
        mesh=mesh,
        in_specs=placed,
        out_specs=(
            P(("dp", "ctx"), "tp", None),
            P(("dp", "ctx"), "tp", None),
            P(("dp", "ctx"), "tp", None),
            P(("dp", "ctx"), "tp", None),
        ),
        check_vma=False,
    )
```

profile of v0, /device:TPU:0, one launch (start us, length us, event | category | flops | bytes accessed | tf_op | source)
XLA Modules:
  0.0 419.5 jit_solution(12107443062514714963)
XLA Ops:
  4.0 8.1 %all-to-all-start = ((bf16[16,16,256]{2,1,0:T(8,128)(2,1)}), bf16[16,16,256]{2,1,0:T(8,128)(2,1)S(1)}, u32[]{:S(2)}, u32[]{:S(2)}) async-start(bf16[16,16,256]{2,1,0:T(8,128)(2,1)} %broadcast_select_fusion.2), calls=%async_computation | async-start | bytes 262144 | tf_op jit(solution)/shard_map/all_to_all | solution.py:49
  25.1 9.8 %all-to-all-done.1 = bf16[16,16,1024]{2,1,0:T(8,128)(2,1)S(1)} async-done(((bf16[16,16,1024]{2,1,0:T(8,128)(2,1)}), bf16[16,16,1024]{2,1,0:T(8,128)(2,1)S(1)}, u32[]{:S(2)}, u32[]{:S(2)}) %all-to-all-start.1) | async-done | bytes 524320 | tf_op jit(solution)/shard_map/all_to_all | solution.py:48
  44.8 175.2 %while.42 = (s32[]{:T(128)}, bf16[256,2,1,128]{3,0,2,1:T(8,128)(2,1)S(1)}, f32[256,1,8]{0,2,1:T(8,128)S(1)}, f32[256,1,8]{0,2,1:T(8,128)S(1)}, f32[256,1,8,128]{...) while((s32[]{:T(128)}, ...), condition=%wide.region_11.13_spmd.clone, body=%wide.region_6.12_spmd.clone.sunk | while | flops 275985472 | bytes 18626248 | solution.py:102
  57.0 7.7 %collective-permute-done = bf16[256,2,1,128]{3,0,2,1:T(8,128)(2,1)S(1)} collective-permute-done((bf16[256,2,1,128]{3,0,2,1:T(8,128)(2,1)S(1)}, bf16[256,2,1,128]{3,0,2,1:T(8,128)(2,1)S(1)}, u32[]{:S(2)}, u32[]{:S(2)}) %collective-permute-start) | collective-permute-done | bytes 131104 | tf_op jit(solution)/shard_map/while/body/eval_jaxpr/ppermute | solution.py:11
  68.6 7.7 %collective-permute-done = bf16[256,2,1,128]{3,0,2,1:T(8,128)(2,1)S(1)} collective-permute-done((bf16[256,2,1,128]{3,0,2,1:T(8,128)(2,1)S(1)}, bf16[256,2,1,128]{3,0,2,1:T(8,128)(2,1)S(1)}, u32[]{:S(2)}, u32[]{:S(2)}) %collective-permute-start) | collective-permute-done | bytes 131104 | tf_op jit(solution)/shard_map/while/body/eval_jaxpr/ppermute | solution.py:11
  80.1 7.7 %collective-permute-done = bf16[256,2,1,128]{3,0,2,1:T(8,128)(2,1)S(1)} collective-permute-done((bf16[256,2,1,128]{3,0,2,1:T(8,128)(2,1)S(1)}, bf16[256,2,1,128]{3,0,2,1:T(8,128)(2,1)S(1)}, u32[]{:S(2)}, u32[]{:S(2)}) %collective-permute-start) | collective-permute-done | bytes 131104 | tf_op jit(solution)/shard_map/while/body/eval_jaxpr/ppermute | solution.py:11
  91.6 7.7 %collective-permute-done = bf16[256,2,1,128]{3,0,2,1:T(8,128)(2,1)S(1)} collective-permute-done((bf16[256,2,1,128]{3,0,2,1:T(8,128)(2,1)S(1)}, bf16[256,2,1,128]{3,0,2,1:T(8,128)(2,1)S(1)}, u32[]{:S(2)}, u32[]{:S(2)}) %collective-permute-start) | collective-permute-done | bytes 131104 | tf_op jit(solution)/shard_map/while/body/eval_jaxpr/ppermute | solution.py:11
  103.2 7.7 %collective-permute-done = bf16[256,2,1,128]{3,0,2,1:T(8,128)(2,1)S(1)} collective-permute-done((bf16[256,2,1,128]{3,0,2,1:T(8,128)(2,1)S(1)}, bf16[256,2,1,128]{3,0,2,1:T(8,128)(2,1)S(1)}, u32[]{:S(2)}, u32[]{:S(2)}) %collective-permute-start) | collective-permute-done | bytes 131104 | tf_op jit(solution)/shard_map/while/body/eval_jaxpr/ppermute | solution.py:11
  114.7 8.1 %collective-permute-done = bf16[256,2,1,128]{3,0,2,1:T(8,128)(2,1)S(1)} collective-permute-done((bf16[256,2,1,128]{3,0,2,1:T(8,128)(2,1)S(1)}, bf16[256,2,1,128]{3,0,2,1:T(8,128)(2,1)S(1)}, u32[]{:S(2)}, u32[]{:S(2)}) %collective-permute-start) | collective-permute-done | bytes 131104 | tf_op jit(solution)/shard_map/while/body/eval_jaxpr/ppermute | solution.py:11
  126.7 8.9 %collective-permute-done = bf16[256,2,1,128]{3,0,2,1:T(8,128)(2,1)S(1)} collective-permute-done((bf16[256,2,1,128]{3,0,2,1:T(8,128)(2,1)S(1)}, bf16[256,2,1,128]{3,0,2,1:T(8,128)(2,1)S(1)}, u32[]{:S(2)}, u32[]{:S(2)}) %collective-permute-start) | collective-permute-done | bytes 131104 | tf_op jit(solution)/shard_map/while/body/eval_jaxpr/ppermute | solution.py:11
  139.4 8.1 %collective-permute-done = bf16[256,2,1,128]{3,0,2,1:T(8,128)(2,1)S(1)} collective-permute-done((bf16[256,2,1,128]{3,0,2,1:T(8,128)(2,1)S(1)}, bf16[256,2,1,128]{3,0,2,1:T(8,128)(2,1)S(1)}, u32[]{:S(2)}, u32[]{:S(2)}) %collective-permute-start) | collective-permute-done | bytes 131104 | tf_op jit(solution)/shard_map/while/body/eval_jaxpr/ppermute | solution.py:11
  151.4 7.7 %collective-permute-done = bf16[256,2,1,128]{3,0,2,1:T(8,128)(2,1)S(1)} collective-permute-done((bf16[256,2,1,128]{3,0,2,1:T(8,128)(2,1)S(1)}, bf16[256,2,1,128]{3,0,2,1:T(8,128)(2,1)S(1)}, u32[]{:S(2)}, u32[]{:S(2)}) %collective-permute-start) | collective-permute-done | bytes 131104 | tf_op jit(solution)/shard_map/while/body/eval_jaxpr/ppermute | solution.py:11
  162.9 7.7 %collective-permute-done = bf16[256,2,1,128]{3,0,2,1:T(8,128)(2,1)S(1)} collective-permute-done((bf16[256,2,1,128]{3,0,2,1:T(8,128)(2,1)S(1)}, bf16[256,2,1,128]{3,0,2,1:T(8,128)(2,1)S(1)}, u32[]{:S(2)}, u32[]{:S(2)}) %collective-permute-start) | collective-permute-done | bytes 131104 | tf_op jit(solution)/shard_map/while/body/eval_jaxpr/ppermute | solution.py:11
  174.4 7.7 %collective-permute-done = bf16[256,2,1,128]{3,0,2,1:T(8,128)(2,1)S(1)} collective-permute-done((bf16[256,2,1,128]{3,0,2,1:T(8,128)(2,1)S(1)}, bf16[256,2,1,128]{3,0,2,1:T(8,128)(2,1)S(1)}, u32[]{:S(2)}, u32[]{:S(2)}) %collective-permute-start) | collective-permute-done | bytes 131104 | tf_op jit(solution)/shard_map/while/body/eval_jaxpr/ppermute | solution.py:11
  186.0 7.7 %collective-permute-done = bf16[256,2,1,128]{3,0,2,1:T(8,128)(2,1)S(1)} collective-permute-done((bf16[256,2,1,128]{3,0,2,1:T(8,128)(2,1)S(1)}, bf16[256,2,1,128]{3,0,2,1:T(8,128)(2,1)S(1)}, u32[]{:S(2)}, u32[]{:S(2)}) %collective-permute-start) | collective-permute-done | bytes 131104 | tf_op jit(solution)/shard_map/while/body/eval_jaxpr/ppermute | solution.py:11
  197.5 7.7 %collective-permute-done = bf16[256,2,1,128]{3,0,2,1:T(8,128)(2,1)S(1)} collective-permute-done((bf16[256,2,1,128]{3,0,2,1:T(8,128)(2,1)S(1)}, bf16[256,2,1,128]{3,0,2,1:T(8,128)(2,1)S(1)}, u32[]{:S(2)}, u32[]{:S(2)}) %collective-permute-start) | collective-permute-done | bytes 131104 | tf_op jit(solution)/shard_map/while/body/eval_jaxpr/ppermute | solution.py:11
  209.1 7.7 %collective-permute-done = bf16[256,2,1,128]{3,0,2,1:T(8,128)(2,1)S(1)} collective-permute-done((bf16[256,2,1,128]{3,0,2,1:T(8,128)(2,1)S(1)}, bf16[256,2,1,128]{3,0,2,1:T(8,128)(2,1)S(1)}, u32[]{:S(2)}, u32[]{:S(2)}) %collective-permute-start) | collective-permute-done | bytes 131104 | tf_op jit(solution)/shard_map/while/body/eval_jaxpr/ppermute | solution.py:11
  241.3 169.2 %while.43 = (s32[]{:T(128)}, bf16[256,2,1,128]{3,0,2,1:T(8,128)(2,1)S(1)}, bf16[256,2,1,128]{3,0,2,1:T(8,128)(2,1)S(1)}, f32[256,1,8,128]{3,0,2,1:T(8,128)S(1)},...) while((s32[]{:T(128)}, ...), condition=%wide.region_16.18_spmd.clone, body=%wide.region_13.17_spmd.clone.sunk | while | flops 675781696 | bytes 16086730 | solution.py:155
  242.2 8.5 %collective-permute-done.1 = bf16[256,2,1,128]{3,0,2,1:T(8,128)(2,1)S(1)} collective-permute-done((bf16[256,2,1,128]{3,0,2,1:T(8,128)(2,1)S(1)}, bf16[256,2,1,128]{3,0,2,1:T(8,128)(2,1)S(1)}, u32[]{:S(2)}, u32[]{:S(2)}) %collective-permute-start.1) | collective-permute-done | bytes 131104 | tf_op jit(solution)/shard_map/while/body/eval_jaxpr/ppermute | solution.py:11
  254.4 9.0 %collective-permute-done.1 = bf16[256,2,1,128]{3,0,2,1:T(8,128)(2,1)S(1)} collective-permute-done((bf16[256,2,1,128]{3,0,2,1:T(8,128)(2,1)S(1)}, bf16[256,2,1,128]{3,0,2,1:T(8,128)(2,1)S(1)}, u32[]{:S(2)}, u32[]{:S(2)}) %collective-permute-start.1) | collective-permute-done | bytes 131104 | tf_op jit(solution)/shard_map/while/body/eval_jaxpr/ppermute | solution.py:11
  266.8 9.0 %collective-permute-done.1 = bf16[256,2,1,128]{3,0,2,1:T(8,128)(2,1)S(1)} collective-permute-done((bf16[256,2,1,128]{3,0,2,1:T(8,128)(2,1)S(1)}, bf16[256,2,1,128]{3,0,2,1:T(8,128)(2,1)S(1)}, u32[]{:S(2)}, u32[]{:S(2)}) %collective-permute-start.1) | collective-permute-done | bytes 131104 | tf_op jit(solution)/shard_map/while/body/eval_jaxpr/ppermute | solution.py:11
  279.2 7.7 %collective-permute-done.1 = bf16[256,2,1,128]{3,0,2,1:T(8,128)(2,1)S(1)} collective-permute-done((bf16[256,2,1,128]{3,0,2,1:T(8,128)(2,1)S(1)}, bf16[256,2,1,128]{3,0,2,1:T(8,128)(2,1)S(1)}, u32[]{:S(2)}, u32[]{:S(2)}) %collective-permute-start.1) | collective-permute-done | bytes 131104 | tf_op jit(solution)/shard_map/while/body/eval_jaxpr/ppermute | solution.py:11
  290.3 7.6 %collective-permute-done.1 = bf16[256,2,1,128]{3,0,2,1:T(8,128)(2,1)S(1)} collective-permute-done((bf16[256,2,1,128]{3,0,2,1:T(8,128)(2,1)S(1)}, bf16[256,2,1,128]{3,0,2,1:T(8,128)(2,1)S(1)}, u32[]{:S(2)}, u32[]{:S(2)}) %collective-permute-start.1) | collective-permute-done | bytes 131104 | tf_op jit(solution)/shard_map/while/body/eval_jaxpr/ppermute | solution.py:11
  301.3 7.6 %collective-permute-done.1 = bf16[256,2,1,128]{3,0,2,1:T(8,128)(2,1)S(1)} collective-permute-done((bf16[256,2,1,128]{3,0,2,1:T(8,128)(2,1)S(1)}, bf16[256,2,1,128]{3,0,2,1:T(8,128)(2,1)S(1)}, u32[]{:S(2)}, u32[]{:S(2)}) %collective-permute-start.1) | collective-permute-done | bytes 131104 | tf_op jit(solution)/shard_map/while/body/eval_jaxpr/ppermute | solution.py:11
  312.3 7.6 %collective-permute-done.1 = bf16[256,2,1,128]{3,0,2,1:T(8,128)(2,1)S(1)} collective-permute-done((bf16[256,2,1,128]{3,0,2,1:T(8,128)(2,1)S(1)}, bf16[256,2,1,128]{3,0,2,1:T(8,128)(2,1)S(1)}, u32[]{:S(2)}, u32[]{:S(2)}) %collective-permute-start.1) | collective-permute-done | bytes 131104 | tf_op jit(solution)/shard_map/while/body/eval_jaxpr/ppermute | solution.py:11
  323.3 7.6 %collective-permute-done.1 = bf16[256,2,1,128]{3,0,2,1:T(8,128)(2,1)S(1)} collective-permute-done((bf16[256,2,1,128]{3,0,2,1:T(8,128)(2,1)S(1)}, bf16[256,2,1,128]{3,0,2,1:T(8,128)(2,1)S(1)}, u32[]{:S(2)}, u32[]{:S(2)}) %collective-permute-start.1) | collective-permute-done | bytes 131104 | tf_op jit(solution)/shard_map/while/body/eval_jaxpr/ppermute | solution.py:11
  334.3 7.6 %collective-permute-done.1 = bf16[256,2,1,128]{3,0,2,1:T(8,128)(2,1)S(1)} collective-permute-done((bf16[256,2,1,128]{3,0,2,1:T(8,128)(2,1)S(1)}, bf16[256,2,1,128]{3,0,2,1:T(8,128)(2,1)S(1)}, u32[]{:S(2)}, u32[]{:S(2)}) %collective-permute-start.1) | collective-permute-done | bytes 131104 | tf_op jit(solution)/shard_map/while/body/eval_jaxpr/ppermute | solution.py:11
  345.3 7.6 %collective-permute-done.1 = bf16[256,2,1,128]{3,0,2,1:T(8,128)(2,1)S(1)} collective-permute-done((bf16[256,2,1,128]{3,0,2,1:T(8,128)(2,1)S(1)}, bf16[256,2,1,128]{3,0,2,1:T(8,128)(2,1)S(1)}, u32[]{:S(2)}, u32[]{:S(2)}) %collective-permute-start.1) | collective-permute-done | bytes 131104 | tf_op jit(solution)/shard_map/while/body/eval_jaxpr/ppermute | solution.py:11
  356.3 7.6 %collective-permute-done.1 = bf16[256,2,1,128]{3,0,2,1:T(8,128)(2,1)S(1)} collective-permute-done((bf16[256,2,1,128]{3,0,2,1:T(8,128)(2,1)S(1)}, bf16[256,2,1,128]{3,0,2,1:T(8,128)(2,1)S(1)}, u32[]{:S(2)}, u32[]{:S(2)}) %collective-permute-start.1) | collective-permute-done | bytes 131104 | tf_op jit(solution)/shard_map/while/body/eval_jaxpr/ppermute | solution.py:11
  367.3 7.6 %collective-permute-done.1 = bf16[256,2,1,128]{3,0,2,1:T(8,128)(2,1)S(1)} collective-permute-done((bf16[256,2,1,128]{3,0,2,1:T(8,128)(2,1)S(1)}, bf16[256,2,1,128]{3,0,2,1:T(8,128)(2,1)S(1)}, u32[]{:S(2)}, u32[]{:S(2)}) %collective-permute-start.1) | collective-permute-done | bytes 131104 | tf_op jit(solution)/shard_map/while/body/eval_jaxpr/ppermute | solution.py:11
  378.3 7.6 %collective-permute-done.1 = bf16[256,2,1,128]{3,0,2,1:T(8,128)(2,1)S(1)} collective-permute-done((bf16[256,2,1,128]{3,0,2,1:T(8,128)(2,1)S(1)}, bf16[256,2,1,128]{3,0,2,1:T(8,128)(2,1)S(1)}, u32[]{:S(2)}, u32[]{:S(2)}) %collective-permute-start.1) | collective-permute-done | bytes 131104 | tf_op jit(solution)/shard_map/while/body/eval_jaxpr/ppermute | solution.py:11
  389.3 7.6 %collective-permute-done.1 = bf16[256,2,1,128]{3,0,2,1:T(8,128)(2,1)S(1)} collective-permute-done((bf16[256,2,1,128]{3,0,2,1:T(8,128)(2,1)S(1)}, bf16[256,2,1,128]{3,0,2,1:T(8,128)(2,1)S(1)}, u32[]{:S(2)}, u32[]{:S(2)}) %collective-permute-start.1) | collective-permute-done | bytes 131104 | tf_op jit(solution)/shard_map/while/body/eval_jaxpr/ppermute | solution.py:11
  (635 shorter events, 178.1 us)
Async XLA Ops:
  4.0 16.1 %all-to-all-start = ((bf16[16,16,256]{2,1,0:T(8,128)(2,1)}), bf16[16,16,256]{2,1,0:T(8,128)(2,1)S(1)}, u32[]{:S(2)}, u32[]{:S(2)}) async-start(bf16[16,16,256]{2,1,0:T(8,128)(2,1)} %broadcast_select_fusion.2), calls=%async_computation | async-start | bytes 262144 | tf_op jit(solution)/shard_map/all_to_all | solution.py:49
  20.1 14.9 %all-to-all-start.1 = ((bf16[16,16,1024]{2,1,0:T(8,128)(2,1)}), bf16[16,16,1024]{2,1,0:T(8,128)(2,1)S(1)}, u32[]{:S(2)}, u32[]{:S(2)}) async-start(bf16[16,16,1024]{2,1,0:T(8,128)(2,1)} %get-tuple-element.804), calls=%async_computation.1 | async-start | bytes 1048576 | tf_op jit(solution)/shard_map/all_to_all | solution.py:48
  35.0 185.8 %all-to-all-start.2 = ((bf16[16,16,1024]{2,1,0:T(8,128)(2,1)}), bf16[16,16,1024]{2,1,0:T(8,128)(2,1)}, u32[]{:S(2)}, u32[]{:S(2)}) async-start(bf16[16,16,1024]{2,1,0:T(8,128)(2,1)} %get-tuple-element.805), calls=%async_computation.2 | async-start | bytes 1048576 | tf_op jit(solution)/shard_map/all_to_all | solution.py:50
  44.8 8.4 %collective-permute-start = (bf16[256,2,1,128]{3,0,2,1:T(8,128)(2,1)S(1)}, bf16[256,2,1,128]{3,0,2,1:T(8,128)(2,1)S(1)}, u32[]{:S(2)}, u32[]{:S(2)}) collective-permute-start(bf16[256,2,1,128]{3,0,2,1:T(8,128)(2,1)S(1)} %get-tuple-element.986), channel_id=1, source_target_pairs={{0,4},{4,8},{8,12},{12,16},{16,20},{20,24},{24,28},{28,32},{32,36}... | collective-permute-start | bytes 393224 | tf_op jit(solution)/shard_map/while/body/eval_jaxpr/ppermute | solution.py:11
  114.1 8.7 %collective-permute-start = (bf16[256,2,1,128]{3,0,2,1:T(8,128)(2,1)S(1)}, bf16[256,2,1,128]{3,0,2,1:T(8,128)(2,1)S(1)}, u32[]{:S(2)}, u32[]{:S(2)}) collective-permute-start(bf16[256,2,1,128]{3,0,2,1:T(8,128)(2,1)S(1)} %get-tuple-element.986), channel_id=1, source_target_pairs={{0,4},{4,8},{8,12},{12,16},{16,20},{20,24},{24,28},{28,32},{32,36}... | collective-permute-start | bytes 393224 | tf_op jit(solution)/shard_map/while/body/eval_jaxpr/ppermute | solution.py:11
  126.1 9.5 %collective-permute-start = (bf16[256,2,1,128]{3,0,2,1:T(8,128)(2,1)S(1)}, bf16[256,2,1,128]{3,0,2,1:T(8,128)(2,1)S(1)}, u32[]{:S(2)}, u32[]{:S(2)}) collective-permute-start(bf16[256,2,1,128]{3,0,2,1:T(8,128)(2,1)S(1)} %get-tuple-element.986), channel_id=1, source_target_pairs={{0,4},{4,8},{8,12},{12,16},{16,20},{20,24},{24,28},{28,32},{32,36}... | collective-permute-start | bytes 393224 | tf_op jit(solution)/shard_map/while/body/eval_jaxpr/ppermute | solution.py:11
  138.8 8.7 %collective-permute-start = (bf16[256,2,1,128]{3,0,2,1:T(8,128)(2,1)S(1)}, bf16[256,2,1,128]{3,0,2,1:T(8,128)(2,1)S(1)}, u32[]{:S(2)}, u32[]{:S(2)}) collective-permute-start(bf16[256,2,1,128]{3,0,2,1:T(8,128)(2,1)S(1)} %get-tuple-element.986), channel_id=1, source_target_pairs={{0,4},{4,8},{8,12},{12,16},{16,20},{20,24},{24,28},{28,32},{32,36}... | collective-permute-start | bytes 393224 | tf_op jit(solution)/shard_map/while/body/eval_jaxpr/ppermute | solution.py:11
  241.4 9.3 %collective-permute-start.1 = (bf16[256,2,1,128]{3,0,2,1:T(8,128)(2,1)S(1)}, bf16[256,2,1,128]{3,0,2,1:T(8,128)(2,1)S(1)}, u32[]{:S(2)}, u32[]{:S(2)}) collective-permute-start(bf16[256,2,1,128]{3,0,2,1:T(8,128)(2,1)S(1)} %get-tuple-element.1033), channel_id=1, source_target_pairs={{0,4},{4,8},{8,12},{12,16},{16,20},{20,24},{24,28},{28,32},{32,36}... | collective-permute-start | bytes 393224 | tf_op jit(solution)/shard_map/while/body/eval_jaxpr/ppermute | solution.py:11
  241.5 12.0 %collective-permute-start.2 = (bf16[256,2,1,128]{3,0,2,1:T(8,128)(2,1)S(1)}, bf16[256,2,1,128]{3,0,2,1:T(8,128)(2,1)S(1)}, u32[]{:S(2)}, u32[]{:S(2)}) collective-permute-start(bf16[256,2,1,128]{3,0,2,1:T(8,128)(2,1)S(1)} %get-tuple-element.1034), channel_id=1, source_target_pairs={{0,4},{4,8},{8,12},{12,16},{16,20},{20,24},{24,28},{28,32},{32,36}... | collective-permute-start | bytes 393224 | tf_op jit(solution)/shard_map/while/body/eval_jaxpr/ppermute | solution.py:11
  253.6 9.8 %collective-permute-start.1 = (bf16[256,2,1,128]{3,0,2,1:T(8,128)(2,1)S(1)}, bf16[256,2,1,128]{3,0,2,1:T(8,128)(2,1)S(1)}, u32[]{:S(2)}, u32[]{:S(2)}) collective-permute-start(bf16[256,2,1,128]{3,0,2,1:T(8,128)(2,1)S(1)} %get-tuple-element.1033), channel_id=1, source_target_pairs={{0,4},{4,8},{8,12},{12,16},{16,20},{20,24},{24,28},{28,32},{32,36}... | collective-permute-start | bytes 393224 | tf_op jit(solution)/shard_map/while/body/eval_jaxpr/ppermute | solution.py:11
  253.7 12.3 %collective-permute-start.2 = (bf16[256,2,1,128]{3,0,2,1:T(8,128)(2,1)S(1)}, bf16[256,2,1,128]{3,0,2,1:T(8,128)(2,1)S(1)}, u32[]{:S(2)}, u32[]{:S(2)}) collective-permute-start(bf16[256,2,1,128]{3,0,2,1:T(8,128)(2,1)S(1)} %get-tuple-element.1034), channel_id=1, source_target_pairs={{0,4},{4,8},{8,12},{12,16},{16,20},{20,24},{24,28},{28,32},{32,36}... | collective-permute-start | bytes 393224 | tf_op jit(solution)/shard_map/while/body/eval_jaxpr/ppermute | solution.py:11
  266.0 9.8 %collective-permute-start.1 = (bf16[256,2,1,128]{3,0,2,1:T(8,128)(2,1)S(1)}, bf16[256,2,1,128]{3,0,2,1:T(8,128)(2,1)S(1)}, u32[]{:S(2)}, u32[]{:S(2)}) collective-permute-start(bf16[256,2,1,128]{3,0,2,1:T(8,128)(2,1)S(1)} %get-tuple-element.1033), channel_id=1, source_target_pairs={{0,4},{4,8},{8,12},{12,16},{16,20},{20,24},{24,28},{28,32},{32,36}... | collective-permute-start | bytes 393224 | tf_op jit(solution)/shard_map/while/body/eval_jaxpr/ppermute | solution.py:11
  266.1 12.3 %collective-permute-start.2 = (bf16[256,2,1,128]{3,0,2,1:T(8,128)(2,1)S(1)}, bf16[256,2,1,128]{3,0,2,1:T(8,128)(2,1)S(1)}, u32[]{:S(2)}, u32[]{:S(2)}) collective-permute-start(bf16[256,2,1,128]{3,0,2,1:T(8,128)(2,1)S(1)} %get-tuple-element.1034), channel_id=1, source_target_pairs={{0,4},{4,8},{8,12},{12,16},{16,20},{20,24},{24,28},{28,32},{32,36}... | collective-permute-start | bytes 393224 | tf_op jit(solution)/shard_map/while/body/eval_jaxpr/ppermute | solution.py:11
  278.4 8.5 %collective-permute-start.1 = (bf16[256,2,1,128]{3,0,2,1:T(8,128)(2,1)S(1)}, bf16[256,2,1,128]{3,0,2,1:T(8,128)(2,1)S(1)}, u32[]{:S(2)}, u32[]{:S(2)}) collective-permute-start(bf16[256,2,1,128]{3,0,2,1:T(8,128)(2,1)S(1)} %get-tuple-element.1033), channel_id=1, source_target_pairs={{0,4},{4,8},{8,12},{12,16},{16,20},{20,24},{24,28},{28,32},{32,36}... | collective-permute-start | bytes 393224 | tf_op jit(solution)/shard_map/while/body/eval_jaxpr/ppermute | solution.py:11
  278.5 11.0 %collective-permute-start.2 = (bf16[256,2,1,128]{3,0,2,1:T(8,128)(2,1)S(1)}, bf16[256,2,1,128]{3,0,2,1:T(8,128)(2,1)S(1)}, u32[]{:S(2)}, u32[]{:S(2)}) collective-permute-start(bf16[256,2,1,128]{3,0,2,1:T(8,128)(2,1)S(1)} %get-tuple-element.1034), channel_id=1, source_target_pairs={{0,4},{4,8},{8,12},{12,16},{16,20},{20,24},{24,28},{28,32},{32,36}... | collective-permute-start | bytes 393224 | tf_op jit(solution)/shard_map/while/body/eval_jaxpr/ppermute | solution.py:11
  289.5 8.4 %collective-permute-start.1 = (bf16[256,2,1,128]{3,0,2,1:T(8,128)(2,1)S(1)}, bf16[256,2,1,128]{3,0,2,1:T(8,128)(2,1)S(1)}, u32[]{:S(2)}, u32[]{:S(2)}) collective-permute-start(bf16[256,2,1,128]{3,0,2,1:T(8,128)(2,1)S(1)} %get-tuple-element.1033), channel_id=1, source_target_pairs={{0,4},{4,8},{8,12},{12,16},{16,20},{20,24},{24,28},{28,32},{32,36}... | collective-permute-start | bytes 393224 | tf_op jit(solution)/shard_map/while/body/eval_jaxpr/ppermute | solution.py:11
  289.6 10.9 %collective-permute-start.2 = (bf16[256,2,1,128]{3,0,2,1:T(8,128)(2,1)S(1)}, bf16[256,2,1,128]{3,0,2,1:T(8,128)(2,1)S(1)}, u32[]{:S(2)}, u32[]{:S(2)}) collective-permute-start(bf16[256,2,1,128]{3,0,2,1:T(8,128)(2,1)S(1)} %get-tuple-element.1034), channel_id=1, source_target_pairs={{0,4},{4,8},{8,12},{12,16},{16,20},{20,24},{24,28},{28,32},{32,36}... | collective-permute-start | bytes 393224 | tf_op jit(solution)/shard_map/while/body/eval_jaxpr/ppermute | solution.py:11
  300.5 8.4 %collective-permute-start.1 = (bf16[256,2,1,128]{3,0,2,1:T(8,128)(2,1)S(1)}, bf16[256,2,1,128]{3,0,2,1:T(8,128)(2,1)S(1)}, u32[]{:S(2)}, u32[]{:S(2)}) collective-permute-start(bf16[256,2,1,128]{3,0,2,1:T(8,128)(2,1)S(1)} %get-tuple-element.1033), channel_id=1, source_target_pairs={{0,4},{4,8},{8,12},{12,16},{16,20},{20,24},{24,28},{28,32},{32,36}... | collective-permute-start | bytes 393224 | tf_op jit(solution)/shard_map/while/body/eval_jaxpr/ppermute | solution.py:11
  300.6 10.9 %collective-permute-start.2 = (bf16[256,2,1,128]{3,0,2,1:T(8,128)(2,1)S(1)}, bf16[256,2,1,128]{3,0,2,1:T(8,128)(2,1)S(1)}, u32[]{:S(2)}, u32[]{:S(2)}) collective-permute-start(bf16[256,2,1,128]{3,0,2,1:T(8,128)(2,1)S(1)} %get-tuple-element.1034), channel_id=1, source_target_pairs={{0,4},{4,8},{8,12},{12,16},{16,20},{20,24},{24,28},{28,32},{32,36}... | collective-permute-start | bytes 393224 | tf_op jit(solution)/shard_map/while/body/eval_jaxpr/ppermute | solution.py:11
  311.5 8.4 %collective-permute-start.1 = (bf16[256,2,1,128]{3,0,2,1:T(8,128)(2,1)S(1)}, bf16[256,2,1,128]{3,0,2,1:T(8,128)(2,1)S(1)}, u32[]{:S(2)}, u32[]{:S(2)}) collective-permute-start(bf16[256,2,1,128]{3,0,2,1:T(8,128)(2,1)S(1)} %get-tuple-element.1033), channel_id=1, source_target_pairs={{0,4},{4,8},{8,12},{12,16},{16,20},{20,24},{24,28},{28,32},{32,36}... | collective-permute-start | bytes 393224 | tf_op jit(solution)/shard_map/while/body/eval_jaxpr/ppermute | solution.py:11
  311.6 10.9 %collective-permute-start.2 = (bf16[256,2,1,128]{3,0,2,1:T(8,128)(2,1)S(1)}, bf16[256,2,1,128]{3,0,2,1:T(8,128)(2,1)S(1)}, u32[]{:S(2)}, u32[]{:S(2)}) collective-permute-start(bf16[256,2,1,128]{3,0,2,1:T(8,128)(2,1)S(1)} %get-tuple-element.1034), channel_id=1, source_target_pairs={{0,4},{4,8},{8,12},{12,16},{16,20},{20,24},{24,28},{28,32},{32,36}... | collective-permute-start | bytes 393224 | tf_op jit(solution)/shard_map/while/body/eval_jaxpr/ppermute | solution.py:11
  322.5 8.4 %collective-permute-start.1 = (bf16[256,2,1,128]{3,0,2,1:T(8,128)(2,1)S(1)}, bf16[256,2,1,128]{3,0,2,1:T(8,128)(2,1)S(1)}, u32[]{:S(2)}, u32[]{:S(2)}) collective-permute-start(bf16[256,2,1,128]{3,0,2,1:T(8,128)(2,1)S(1)} %get-tuple-element.1033), channel_id=1, source_target_pairs={{0,4},{4,8},{8,12},{12,16},{16,20},{20,24},{24,28},{28,32},{32,36}... | collective-permute-start | bytes 393224 | tf_op jit(solution)/shard_map/while/body/eval_jaxpr/ppermute | solution.py:11
  322.6 10.9 %collective-permute-start.2 = (bf16[256,2,1,128]{3,0,2,1:T(8,128)(2,1)S(1)}, bf16[256,2,1,128]{3,0,2,1:T(8,128)(2,1)S(1)}, u32[]{:S(2)}, u32[]{:S(2)}) collective-permute-start(bf16[256,2,1,128]{3,0,2,1:T(8,128)(2,1)S(1)} %get-tuple-element.1034), channel_id=1, source_target_pairs={{0,4},{4,8},{8,12},{12,16},{16,20},{20,24},{24,28},{28,32},{32,36}... | collective-permute-start | bytes 393224 | tf_op jit(solution)/shard_map/while/body/eval_jaxpr/ppermute | solution.py:11
  333.5 8.4 %collective-permute-start.1 = (bf16[256,2,1,128]{3,0,2,1:T(8,128)(2,1)S(1)}, bf16[256,2,1,128]{3,0,2,1:T(8,128)(2,1)S(1)}, u32[]{:S(2)}, u32[]{:S(2)}) collective-permute-start(bf16[256,2,1,128]{3,0,2,1:T(8,128)(2,1)S(1)} %get-tuple-element.1033), channel_id=1, source_target_pairs={{0,4},{4,8},{8,12},{12,16},{16,20},{20,24},{24,28},{28,32},{32,36}... | collective-permute-start | bytes 393224 | tf_op jit(solution)/shard_map/while/body/eval_jaxpr/ppermute | solution.py:11
  333.6 10.9 %collective-permute-start.2 = (bf16[256,2,1,128]{3,0,2,1:T(8,128)(2,1)S(1)}, bf16[256,2,1,128]{3,0,2,1:T(8,128)(2,1)S(1)}, u32[]{:S(2)}, u32[]{:S(2)}) collective-permute-start(bf16[256,2,1,128]{3,0,2,1:T(8,128)(2,1)S(1)} %get-tuple-element.1034), channel_id=1, source_target_pairs={{0,4},{4,8},{8,12},{12,16},{16,20},{20,24},{24,28},{28,32},{32,36}... | collective-permute-start | bytes 393224 | tf_op jit(solution)/shard_map/while/body/eval_jaxpr/ppermute | solution.py:11
  344.5 8.4 %collective-permute-start.1 = (bf16[256,2,1,128]{3,0,2,1:T(8,128)(2,1)S(1)}, bf16[256,2,1,128]{3,0,2,1:T(8,128)(2,1)S(1)}, u32[]{:S(2)}, u32[]{:S(2)}) collective-permute-start(bf16[256,2,1,128]{3,0,2,1:T(8,128)(2,1)S(1)} %get-tuple-element.1033), channel_id=1, source_target_pairs={{0,4},{4,8},{8,12},{12,16},{16,20},{20,24},{24,28},{28,32},{32,36}... | collective-permute-start | bytes 393224 | tf_op jit(solution)/shard_map/while/body/eval_jaxpr/ppermute | solution.py:11
  344.6 10.9 %collective-permute-start.2 = (bf16[256,2,1,128]{3,0,2,1:T(8,128)(2,1)S(1)}, bf16[256,2,1,128]{3,0,2,1:T(8,128)(2,1)S(1)}, u32[]{:S(2)}, u32[]{:S(2)}) collective-permute-start(bf16[256,2,1,128]{3,0,2,1:T(8,128)(2,1)S(1)} %get-tuple-element.1034), channel_id=1, source_target_pairs={{0,4},{4,8},{8,12},{12,16},{16,20},{20,24},{24,28},{28,32},{32,36}... | collective-permute-start | bytes 393224 | tf_op jit(solution)/shard_map/while/body/eval_jaxpr/ppermute | solution.py:11
  355.6 10.9 %collective-permute-start.2 = (bf16[256,2,1,128]{3,0,2,1:T(8,128)(2,1)S(1)}, bf16[256,2,1,128]{3,0,2,1:T(8,128)(2,1)S(1)}, u32[]{:S(2)}, u32[]{:S(2)}) collective-permute-start(bf16[256,2,1,128]{3,0,2,1:T(8,128)(2,1)S(1)} %get-tuple-element.1034), channel_id=1, source_target_pairs={{0,4},{4,8},{8,12},{12,16},{16,20},{20,24},{24,28},{28,32},{32,36}... | collective-permute-start | bytes 393224 | tf_op jit(solution)/shard_map/while/body/eval_jaxpr/ppermute | solution.py:11
  366.6 10.9 %collective-permute-start.2 = (bf16[256,2,1,128]{3,0,2,1:T(8,128)(2,1)S(1)}, bf16[256,2,1,128]{3,0,2,1:T(8,128)(2,1)S(1)}, u32[]{:S(2)}, u32[]{:S(2)}) collective-permute-start(bf16[256,2,1,128]{3,0,2,1:T(8,128)(2,1)S(1)} %get-tuple-element.1034), channel_id=1, source_target_pairs={{0,4},{4,8},{8,12},{12,16},{16,20},{20,24},{24,28},{28,32},{32,36}... | collective-permute-start | bytes 393224 | tf_op jit(solution)/shard_map/while/body/eval_jaxpr/ppermute | solution.py:11
  377.6 10.9 %collective-permute-start.2 = (bf16[256,2,1,128]{3,0,2,1:T(8,128)(2,1)S(1)}, bf16[256,2,1,128]{3,0,2,1:T(8,128)(2,1)S(1)}, u32[]{:S(2)}, u32[]{:S(2)}) collective-permute-start(bf16[256,2,1,128]{3,0,2,1:T(8,128)(2,1)S(1)} %get-tuple-element.1034), channel_id=1, source_target_pairs={{0,4},{4,8},{8,12},{12,16},{16,20},{20,24},{24,28},{28,32},{32,36}... | collective-permute-start | bytes 393224 | tf_op jit(solution)/shard_map/while/body/eval_jaxpr/ppermute | solution.py:11
  388.6 10.9 %collective-permute-start.2 = (bf16[256,2,1,128]{3,0,2,1:T(8,128)(2,1)S(1)}, bf16[256,2,1,128]{3,0,2,1:T(8,128)(2,1)S(1)}, u32[]{:S(2)}, u32[]{:S(2)}) collective-permute-start(bf16[256,2,1,128]{3,0,2,1:T(8,128)(2,1)S(1)} %get-tuple-element.1034), channel_id=1, source_target_pairs={{0,4},{4,8},{8,12},{12,16},{16,20},{20,24},{24,28},{28,32},{32,36}... | collective-permute-start | bytes 393224 | tf_op jit(solution)/shard_map/while/body/eval_jaxpr/ppermute | solution.py:11
  399.6 10.9 %collective-permute-start.2 = (bf16[256,2,1,128]{3,0,2,1:T(8,128)(2,1)S(1)}, bf16[256,2,1,128]{3,0,2,1:T(8,128)(2,1)S(1)}, u32[]{:S(2)}, u32[]{:S(2)}) collective-permute-start(bf16[256,2,1,128]{3,0,2,1:T(8,128)(2,1)S(1)} %get-tuple-element.1034), channel_id=1, source_target_pairs={{0,4},{4,8},{8,12},{12,16},{16,20},{20,24},{24,28},{28,32},{32,36}... | collective-permute-start | bytes 393224 | tf_op jit(solution)/shard_map/while/body/eval_jaxpr/ppermute | solution.py:11
  (63 other events, 250.7 us)
where the time goes:
time: 421 us; the launch traced here: 419 us
  waiting for transfers between devices  253 us (60%)
  matrix products  68.4 us (16%)
  local copies, waits for them, and re-layouts  42.2 us (10%)
  other arithmetic  31.2 us (7%)
  starting transfers between devices  20.4 us (5%)
    ppermute x46, waiting for transfers between devices, passed_along(): lax.ppermute(array, axis, [(i, (i + by) % size) for i in range(size)])  240 us
    while x105, local copies, waits for them, and re-layouts  17.6 us
    dot_general x16, matrix products, forward_tile(): jnp.einsum('tgru,ugd->tgrd', weights.astype(jnp.bfloat16), pair_rows[:, 1...  17.1 us
    dot_general x16, matrix products, backward_tile(): jnp.einsum('tgru,ugd->tgrd', slopes, pair_rows[:, 0], preferred_element_t...  10.9 us
    all_to_all x1, waiting for transfers between devices, on_device(): lax.all_to_all(arrange(query), 'ctx', split_axis=0, concat_axis=0, tiled=...  9.85 us
    dot_general x15, matrix products, backward_tile(): jnp.einsum('tgrd,ugd->tgru', query_rows_all, pair_rows[:, 0], preferred_e...  8.66 us
  transfers between devices with their start and end apart: 49, of which 35 were waited for; matrix products, arithmetic and copies ran while one was open for 24% of the time, Pallas kernels for 0%

commit v1 on v0

v1 whole, which is shorter than its diff:
```python
import functools

import jax
import jax.numpy as jnp
from jax import lax
from jax.experimental import pallas as pl
from jax.experimental.pallas import tpu as pltpu
from jax.sharding import PartitionSpec as P

NEG = -1e30
LOG2E = 1.4426950408889634
NT = (((1,), (1,)), ((), ()))
NN = (((1,), (0,)), ((), ()))


def dot(a, b, dims):
    return lax.dot_general(a, b, dims, preferred_element_type=jnp.float32)


def folded(x, op):
    return op(x.reshape(x.shape[0] // 8, 8, x.shape[1]), axis=0)


def attention_kernel(tile, scale, me, lengths, owners, q_ref, g_ref, kv_ref,
                     out_ref, dq_ref, dkv_ref,
                     kvt, acc, pair, s_buf, d_buf, o_acc, dq_acc):
    if me is None:
        me = lax.axis_index("ctx")
    shards, rows, width = q_ref.shape
    keys = kv_ref.shape[0]
    ndocs = lengths.shape[0]
    shard_rows = keys // shards
    block = shard_rows // shards
    heads = rows // block
    per_scale = scale * LOG2E

    acc[...] = jnp.zeros_like(acc)
    pair[...] = jnp.zeros_like(pair)

    @pl.loop(0, keys // 128)
    def _(b):
        at = pl.ds(pl.multiple_of(b * 128, 128), 128)
        kvt[0:width, at] = kv_ref[at, 0:width].T
        kvt[width:2 * width, at] = kv_ref[at, width:2 * width].T

    token = lax.broadcasted_iota(jnp.int32, (1, rows), 1) // heads
    key_index = lax.broadcasted_iota(jnp.int32, (tile, rows), 0)

    @pl.loop(0, shards)
    def _(j):
        slot = jnp.int32(0)
        for s in range(shards):
            slot = slot + jnp.where(owners[j, s] == me, s, 0)
        first = j * shard_rows + slot * block
        pos = first + token
        start = jnp.zeros_like(pos)
        low = jnp.int32(0)
        end = jnp.int32(0)
        for d in range(ndocs):
            end = end + lengths[d]
            start = jnp.where(end <= pos, end, start)
            low = jnp.where(end <= first, end, low)
        base = (low // 128) * 128
        count = (first + block - base + tile - 1) // tile

        pair[0:rows, 0:width] = q_ref[j]
        pair[rows:2 * rows, width:2 * width] = g_ref[j]

        def window(t):
            want = base + t * tile
            return want, pl.multiple_of(jnp.minimum(want, keys - tile), 128)

        def scores(t, peak):
            want, at = window(t)
            both = dot(kv_ref[pl.ds(at, tile), :], pair[...], NT)
            lower = jnp.maximum(start, want) - at
            allowed = (key_index >= lower) & (key_index <= pos - at)
            s = jnp.where(allowed, both[:, 0:rows], NEG)
            here = pl.ds(pl.multiple_of(t * tile, tile), tile)
            s_buf[here, :] = s
            d_buf[here, :] = both[:, rows:2 * rows]
            return jnp.maximum(peak, folded(s, jnp.max))

        peak = lax.fori_loop(0, count, scores, jnp.full((8, rows), NEG, jnp.float32))
        peak = jnp.max(peak, axis=0, keepdims=True)

        def weights(t, sums):
            here = pl.ds(pl.multiple_of(t * tile, tile), tile)
            p = jnp.exp2((s_buf[here, :] - peak) * per_scale)
            s_buf[here, :] = p
            return sums[0] + folded(p, jnp.sum), sums[1] + folded(p * d_buf[here, :], jnp.sum)

        zero = jnp.zeros((8, rows), jnp.float32)
        total, delta = lax.fori_loop(0, count, weights, (zero, zero))
        inverse = 1.0 / jnp.sum(total, axis=0, keepdims=True)
        delta = jnp.sum(delta, axis=0, keepdims=True) * inverse

        o_acc[...] = jnp.zeros_like(o_acc)
        dq_acc[...] = jnp.zeros_like(dq_acc)

        @pl.loop(0, count)
        def _(t):
            _, at = window(t)
            here = pl.ds(pl.multiple_of(t * tile, tile), tile)
            probs = s_buf[here, :] * inverse
            slopes = probs * (d_buf[here, :] - delta)
            probs = probs.astype(jnp.bfloat16)
            slopes = slopes.astype(jnp.bfloat16)
            span = pl.ds(at, tile)
            acc[span, :] += dot(jnp.concatenate([slopes, probs], axis=1), pair[...], NN)
            dq_acc[...] += dot(kvt[0:width, span], slopes, NN)
            o_acc[...] += dot(kvt[width:2 * width, span], probs, NN)

        out_ref[j] = o_acc[...].T.astype(jnp.bfloat16)
        dq_ref[j] = (dq_acc[...] * scale).T.astype(jnp.bfloat16)

    @pl.loop(0, shards)
    def _(j):
        for s in range(shards):
            rows_at = pl.ds(pl.multiple_of(j * shard_rows + s * block, block), block)
            part = acc[rows_at, :]
            owner = owners[j, s]
            dkv_ref[owner, j, :, 0:width] = (part[:, 0:width] * scale).astype(jnp.bfloat16)
            dkv_ref[owner, j, :, width:2 * width] = part[:, width:2 * width].astype(jnp.bfloat16)


def attention(q, g, kv, lengths, owners, me=None, tile=512, interpret=False):
    shards, rows, width = q.shape
    keys = kv.shape[0]
    block = keys // shards // shards
    reach = -(-(2048 + block + 128) // tile) * tile
    smem = pl.BlockSpec(memory_space=pltpu.SMEM)
    vmem = pl.BlockSpec(memory_space=pltpu.VMEM)
    return pl.pallas_call(
        functools.partial(attention_kernel, tile, width ** -0.5, me),
        out_shape=(
            jax.ShapeDtypeStruct((shards, rows, width), jnp.bfloat16),
            jax.ShapeDtypeStruct((shards, rows, width), jnp.bfloat16),
            jax.ShapeDtypeStruct((shards, shards, block, 2 * width), jnp.bfloat16),
        ),
        in_specs=[smem, smem, vmem, vmem, vmem],
        out_specs=(vmem, vmem, vmem),
        scratch_shapes=[
            pltpu.VMEM((2 * width, keys), jnp.bfloat16),
            pltpu.VMEM((keys, 2 * width), jnp.float32),
            pltpu.VMEM((2 * rows, 2 * width), jnp.bfloat16),
            pltpu.VMEM((reach, rows), jnp.float32),
            pltpu.VMEM((reach, rows), jnp.float32),
            pltpu.VMEM((width, rows), jnp.float32),
            pltpu.VMEM((width, rows), jnp.float32),
        ],
        compiler_params=pltpu.CompilerParams(vmem_limit_bytes=40 << 20),
        interpret=interpret,
    )(lengths, owners, q, g, kv)


def on_device(query, keys, values, output_gradient, doc_lengths, block_owner):
    shards = lax.axis_size("ctx")
    me = lax.axis_index("ctx")
    local, heads, width = query.shape
    block = local // shards
    targets = lax.dynamic_index_in_dim(block_owner, me, 0, keepdims=False)
    ids = jnp.arange(shards, dtype=jnp.int32)
    order = jnp.sum((targets[:, None] == ids[None, :]).astype(jnp.int32) * ids[:, None], axis=0)

    def arrange(source):
        moved = jnp.take(source.reshape(shards, block * heads, width), order, axis=0)
        return lax.all_to_all(moved, "ctx", split_axis=0, concat_axis=0, tiled=True)

    kv = lax.all_gather(jnp.concatenate([keys[:, 0], values[:, 0]], axis=1), "ctx", tiled=True)
    out, dq, dkv = attention(arrange(query), arrange(output_gradient), kv, doc_lengths, block_owner)
    dkv = lax.psum_scatter(dkv, "ctx", scatter_dimension=0, tiled=True).reshape(local, 2 * width)
    return (
        out.reshape(local, heads, width),
        dq.reshape(local, heads, width),
        dkv[:, None, :width],
        dkv[:, None, width:],
    )


def solution(mesh):
    rows = P(("dp", "ctx"), "tp", None)
    return jax.shard_map(
        on_device,
        mesh=mesh,
        in_specs=(rows, rows, rows, rows, P("dp"), P("dp", None)),
        out_specs=(rows, rows, rows, rows),
        check_vma=False,
    )
```

time: 421 us -> 175 us (0.42)
  waiting for transfers between devices: 253 us -> 90.6 us
  matrix products: 68.4 us -> 0 us
  local copies, waits for them, and re-layouts: 42.2 us -> 6.18 us
  blocking collectives: 0 us -> 33.8 us
  other arithmetic: 31.2 us -> 1.88 us
  Pallas kernels: 0 us -> 27.9 us
  starting transfers between devices: 20.4 us -> 0.08 us
  between operations: 1.02 us -> 14.1 us
    ppermute x46 -> x0, waiting for transfers between devices: 240 us -> none  [passed_along(): lax.ppermute(array, axis, [(i, (i + by) % size) for i in range(size)])]
    unnamed x0 -> x3, waiting for transfers between devices: none -> 76.3 us
    dot_general x111 -> x0, matrix products: 68.4 us -> none  [the longest x16 17.1 us: forward_tile(): jnp.einsum('tgru,ugd->tgrd', weights.astype(jnp.bfloat16), pair_rows[:, 1...]
    all_to_all x0 -> x2, blocking collectives: none -> 33.8 us  [arrange(): return lax.all_to_all(moved, 'ctx', split_axis=0, concat_axis=0, tiled=True)]
    pallas_call x0 -> x1, Pallas kernels: none -> 27.9 us  [attention(): pl.pallas_call(functools.partial(attention_kernel, tile, width ** (-0.5),...]
    while x106 -> x0, local copies, waits for them, and re-layouts: 19 us -> none
    all_to_all x3 -> x0, starting transfers between devices: 16.3 us -> none  [the longest x1 8.13 us: on_device(): lax.all_to_all(arrange(loaded_pairs), 'ctx', split_axis=0, concat_axis=0,...]
    reduce_sum x50 -> x1, other arithmetic: 14.7 us -> 0.09 us  [on_device(): jnp.sum((targets[:, None] == ids[None, :]).astype(jnp.int32) * ids[:, Non...]
  transfers between devices with their start and end apart: 49 -> 2, of which waited for: 35 -> 2; matrix products, arithmetic and copies ran while one was open for 24% -> 2% of each run, Pallas kernels for 0% -> 0%
where the time goes in v1:
time: 175 us
  waiting for transfers between devices  90.6 us (52%)
  blocking collectives  33.8 us (19%)
  Pallas kernels  27.9 us (16%)
  between operations  14.1 us (8%)
  local copies, waits for them, and re-layouts  6.18 us (4%)
  other arithmetic  1.88 us (1%)
    unnamed x3, waiting for transfers between devices  76.3 us
    all_to_all x2, blocking collectives, arrange(): return lax.all_to_all(moved, 'ctx', split_axis=0, concat_axis=0, tiled=True)  33.8 us
    pallas_call x1, Pallas kernels, attention(): pl.pallas_call(functools.partial(attention_kernel, tile, width ** (-0.5),...  27.9 us
    all_gather x1, waiting for transfers between devices, on_device(): lax.all_gather(jnp.concatenate([keys[:, 0], values[:, 0]], axis=1), 'ctx'...  14.3 us
  transfers between devices with their start and end apart: 2, of which 2 were waited for; matrix products, arithmetic and copies ran while one was open for 2% of the time, Pallas kernels for 0%

profile of v1, /device:TPU:0, one launch (start us, length us, event | category | flops | bytes accessed | tf_op | source)
XLA Modules:
  0.0 174.6 jit_solution(13007825863147084943)
XLA Ops:
  7.2 0.0 copy-start
  7.2 0.0 all-gather.2.cloned.1.call-start
  7.2 1.6 pad_maximum_fusion
  8.8 0.0 all-gather.2.cloned.1.call-update
  8.8 0.0 reduce-scatter.4.cloned.1.call-start
  8.9 0.7 dynamic-slice_bitcast_fusion
  9.6 0.1 select_reduce_fusion
  9.7 0.0 copy-done
  9.7 0.6 gather_fusion.1
  10.4 1.7 gather_fusion
  12.1 0.0 copy-start.2
  12.1 0.0 copy-start.3
  12.1 0.2 broadcast_select_fusion
  12.3 20.3 %all_to_all.10.g_ref = bf16[16,128,128]{2,1,0:T(8,128)(2,1)S(1)} all-to-all(bf16[16,128,128]{2,1,0:T(8,128)(2,1)S(1)} %get-tuple-element.13), channel_id=1, replica_groups=mesh['dp'=2,'ctx'=16,'tp'=4] {'ctx'}, dimensions={0} | all-to-all | bytes 1048576 | tf_op jit(solution)/shard_map/all_to_all | solution.py:168
  32.5 13.6 %all_to_all.11.q_ref = bf16[16,128,128]{2,1,0:T(8,128)(2,1)S(1)} all-to-all(bf16[16,128,128]{2,1,0:T(8,128)(2,1)S(1)} %get-tuple-element.14), channel_id=1, replica_groups=mesh['dp'=2,'ctx'=16,'tp'=4] {'ctx'}, dimensions={0} | all-to-all | bytes 1048576 | tf_op jit(solution)/shard_map/all_to_all | solution.py:168
  46.1 14.3 %all-gather.2.cloned.1.call-done.kv_ref = bf16[4096,256]{1,0:T(8,128)(2,1)} async-done(((bf16[256,256]{1,0:T(8,128)(2,1)}), bf16[4096,256]{1,0:T(8,128)(2,1)}) %all-gather.2.cloned.1.call-update) | async-done | bytes 2097168 | tf_op jit(solution)/shard_map/all_gather | solution.py:170
  60.4 0.0 copy-done.2
  60.4 0.0 copy-done.3
  60.4 0.0 copy-start.1
  60.4 1.6 copy-done.1
  62.0 27.9 %shard_map.93 = (bf16[16,128,128]{2,1,0:T(8,128)(2,1)}, bf16[16,128,128]{2,1,0:T(8,128)(2,1)}, bf16[16,16,16,256]{3,2,1,0:T(8,128)(2,1)}) custom-call(s32[8]{0:T(128)S(1)} %copy-done.3, s32[16,16]{1,0:T(8,128)S(1)} %copy-done.2, bf16[16,128,128]{2,1,0:T(8,128)(2,1)S(1)} %all_to_all.11.q_ref, bf16[16,128,128]{2,1,0:T(8,128)(2,1)S(1)} %all_to_all.10.g_ref, ...), custom_call_target="tpu_custom_call" | custom-call | tf_op jit(solution)/shard_map/pallas_call | solution.py:134
  89.9 0.0 reduce-scatter.4.cloned.1.call-update
  90.0 76.3 %reduce-scatter.4.cloned.1.call-done = bf16[1,16,16,256]{3,2,1,0:T(8,128)(2,1)} async-done(((bf16[16,16,16,256]{3,2,1,0:T(8,128)(2,1)}), bf16[1,16,16,256]{3,2,1,0:T(8,128)(2,1)}) %reduce-scatter.4.cloned.1.call-update) | async-done | bytes 131088
  166.2 1.5 slice_bitcast_fusion
  (3 shorter events, 0.0 us)
Async XLA Ops:
  7.2 2.5 %copy-start = (bf16[256,8,128]{2,1,0:T(8,128)(2,1)S(1)}, bf16[256,8,128]{2,1,0:T(8,128)(2,1)}, u32[]{:S(2)}) copy-start(bf16[256,8,128]{2,1,0:T(8,128)(2,1)} %param.11) | copy-start | bytes 1572868
  7.2 53.2 %all-gather.2.cloned.1.call-start = ((), (), s32[]{:S(2)}) async-start(), calls=%async_computation.3 | async-start | bytes 2228224 | tf_op jit(solution)/shard_map/all_gather | solution.py:170
  8.8 157.4 %reduce-scatter.4.cloned.1.call-start = ((), (), s32[]{:S(2)}) async-start(), calls=%async_computation.4 | async-start | bytes 2228224
  12.1 48.3 %copy-start.2 = (s32[16,16]{1,0:T(8,128)S(1)}, s32[16,16]{1,0:T(8,128)}, u32[]{:S(2)}) copy-start(s32[16,16]{1,0:T(8,128)} %owners.1) | copy-start | bytes 3076
  12.1 48.3 %copy-start.3 = (s32[8]{0:T(128)S(1)}, s32[8]{0:T(128)}, u32[]{:S(2)}) copy-start(s32[8]{0:T(128)} %lengths.1) | copy-start | bytes 100
  60.4 1.6 copy-start.1
Sparse Core Ops, SparseCore 0:
  10.7 49.6 all-gather.1
  90.1 76.1 reduce-scatter.3

commit v2 on v1

--- a/solution.py
+++ b/solution.py
@@ -21,13 +21,328 @@
     return op(x.reshape(x.shape[0] // 8, 8, x.shape[1]), axis=0)
 
 
-def attention_kernel(tile, scale, me, lengths, owners, q_ref, g_ref, kv_ref,
-                     out_ref, dq_ref, dkv_ref,
+SIDE = 4
+MESH_AXIS = "ctx"
+
+
+def coordinates():
+    me = lax.axis_index(MESH_AXIS)
+    return lax.div(me, SIDE), lax.rem(me, SIDE)
+
+
+def device_at(dz, dy):
+    z, y = coordinates()
+    return lax.rem(z + dz + SIDE, SIDE) * SIDE + lax.rem(y + dy + SIDE, SIDE)
+
+
+def greet(offsets):
+    barrier = pltpu.get_barrier_semaphore()
+    for dz, dy in offsets:
+        pl.semaphore_signal(barrier, inc=1, device_id={MESH_AXIS: device_at(dz, dy)},
+                            device_id_type=pl.DeviceIdType.MESH)
+    pl.semaphore_wait(barrier, len(offsets))
+
+
+class Copies:
+    def __init__(self, send_sems, recv_sems):
+        self.send_sems, self.recv_sems, self.sent = send_sems, recv_sems, []
+
+    def make(self, n, src, dst, target):
+        return pltpu.make_async_remote_copy(
+            src_ref=src, dst_ref=dst, send_sem=self.send_sems.at[n], recv_sem=self.recv_sems.at[n],
+            device_id={MESH_AXIS: target}, device_id_type=pl.DeviceIdType.MESH)
+
+    def send(self, n, src, dst, target):
+        copy = self.make(n, src, dst, target)
+        copy.start()
+        self.sent.append(copy)
+
+    def arrived(self, n, dst):
+        self.make(n, dst, dst, device_at(0, 1)).wait_recv()
+
+    def finish(self):
+        for copy in self.sent:
+            copy.wait_send()
+
+
+OFFSETS = [(dz, dy) for dz in (0, 1, 2, 3) for dy in (0, 1, 2, 3) if (dz, dy) != (0, 0)]
+
+
+class Spread:
+    def __init__(self, first_is_y, own, blocks, copies, base):
+        self.first_is_y, self.own, self.blocks, self.copies, self.base = first_is_y, own, blocks, copies, base
+        self.half = blocks.shape[1] // 2
+
+    def block(self, a, b):
+        return device_at(b, a) if self.first_is_y else device_at(a, b)
+
+    def part(self, a, b, half):
+        block = self.blocks.at[self.block(a, b)]
+        return block if half is None else block.at[pl.ds(half * self.half, self.half)]
+
+    def number(self, stage, a, kind):
+        return self.base + (kind if stage == 1 else 4 + 4 * (a % SIDE) + kind)
+
+    def send(self, stage, a, kind, src, part):
+        step = 1 if kind in (0, 2) else -1
+        target = self.block(step, 0) if stage == 1 else self.block(0, step)
+        self.copies.send(self.number(stage, a, kind), src, part, target)
+
+    def start(self):
+        me = self.part(0, 0, None)
+        for stage in (1, 2):
+            for kind in (0, 1):
+                self.send(stage, 0, kind, self.own, me)
+
+    def got(self, stage, a, kind):
+        along = {0: -1, 1: 1, 2: 2, 3: 2}[kind]
+        half = {0: None, 1: None, 2: 0, 3: 1}[kind]
+        part = self.part(along, 0, half) if stage == 1 else self.part(a, along, half)
+        self.copies.arrived(self.number(stage, a, kind), part)
+
+    def onward(self, stage, a, kind):
+        along = -1 if kind == 0 else 1
+        half = kind
+        part = self.part(along, 0, half) if stage == 1 else self.part(a, along, half)
+        self.send(stage, a, kind + 2, part, part)
+
+    def second(self, a):
+        part = self.part(a, 0, None)
+        for kind in (0, 1):
+            self.send(2, a, kind, part, part)
+
+
+def exchange_kernel(owners, q_ref, g_ref, k_ref, v_ref, qg_out, k_out, v_out,
+                    staging, send_sems, recv_sems):
+    me = lax.axis_index(MESH_AXIS)
+    rows = q_ref.shape[1]
+    copies = Copies(send_sems, recv_sems)
+    k_spread = Spread(True, k_ref, k_out, copies, 0)
+    v_spread = Spread(False, v_ref, v_out, copies, 20)
+    spreads = (k_spread, v_spread)
+
+    greet(OFFSETS)
+    for spread in spreads:
+        spread.start()
+    k_out[me] = k_ref[...]
+    v_out[me] = v_ref[...]
+
+    def slot_for(target):
+        slot = jnp.int32(0)
+        for s in range(SIDE * SIDE):
+            slot = jnp.where(owners[me, s] == target, s, slot)
+        return slot
+
+    def reassign(items):
+        for n in items:
+            target = device_at(*OFFSETS[n])
+            slot = slot_for(target)
+            staging[n, 0:rows] = q_ref[slot]
+            staging[n, rows:2 * rows] = g_ref[slot]
+            copies.send(40 + n, staging.at[n], qg_out.at[me], target)
+
+    far = sorted(range(15), key=lambda n: -sum(min(d, SIDE - d) for d in OFFSETS[n]))
+    reassign(far[:5])
+    for kind in (0, 1):
+        for spread in spreads:
+            spread.got(1, 0, kind)
+            spread.onward(1, 0, kind)
+            spread.second(-1 if kind == 0 else 1)
+    reassign(far[5:10])
+    for spread in spreads:
+        spread.got(1, 0, 2)
+        spread.got(1, 0, 3)
+        spread.second(2)
+    for kind in (0, 1):
+        for spread in spreads:
+            spread.got(2, 0, kind)
+            spread.onward(2, 0, kind)
+    reassign(far[10:])
+    slot = slot_for(me)
+    qg_out[me, 0:rows] = q_ref[slot]
+    qg_out[me, rows:2 * rows] = g_ref[slot]
+    for a in (-1, 1, 2):
+        for kind in (0, 1):
+            for spread in spreads:
+                spread.got(2, a, kind)
+                spread.onward(2, a, kind)
+    for a in (0, -1, 1, 2):
+        for kind in (2, 3):
+            for spread in spreads:
+                spread.got(2, a, kind)
+    for n in far:
+        dz, dy = OFFSETS[n]
+        copies.arrived(40 + n, qg_out.at[device_at(-dz, -dy)])
+    copies.finish()
+
+
+def exchange(owners, q, g, k, v):
+    shards, rows, width = q.shape
+    local = k.shape[0]
+    smem = pl.BlockSpec(memory_space=pltpu.SMEM)
+    vmem = pl.BlockSpec(memory_space=pltpu.VMEM)
+    bf16 = jnp.bfloat16
+    return pl.pallas_call(
+        exchange_kernel,
+        out_shape=(
+            jax.ShapeDtypeStruct((shards, 2 * rows, width), bf16),
+            jax.ShapeDtypeStruct((shards, local, width), bf16),
+            jax.ShapeDtypeStruct((shards, local, width), bf16),
+        ),
+        in_specs=[smem, vmem, vmem, vmem, vmem],
+        out_specs=(vmem, vmem, vmem),
+        scratch_shapes=[
+            pltpu.VMEM((shards - 1, 2 * rows, width), bf16),
+            pltpu.SemaphoreType.DMA((55,)),
+            pltpu.SemaphoreType.DMA((55,)),
+        ],
+        compiler_params=pltpu.CompilerParams(
+            collective_id=0, has_side_effects=True, vmem_limit_bytes=24 << 20),
+    )(owners, q, g, k, v)
+
+
+class Collect:
+    PLUS, MINUS = (2, 0), (1, 3)
+
+    def __init__(self, first_is_y, blocks, out, copies, base, passing, joined, left, right,
+                 sums, own_sum, passing2, joined2, left2, right2):
+        self.first_is_y, self.blocks, self.out, self.copies, self.base = first_is_y, blocks, out, copies, base
+        self.passing, self.joined, self.left, self.right = passing, joined, left, right
+        self.sums, self.own_sum = sums, own_sum
+        self.passing2, self.joined2, self.left2, self.right2 = passing2, joined2, left2, right2
+        self.half = out.shape[0] // 2
+
+    def device(self, a, b):
+        return device_at(b, a) if self.first_is_y else device_at(a, b)
+
+    def begin(self):
+        for b in (2, 1, 0, 3):
+            step = 1 if b in self.PLUS else -1
+            self.copies.send(self.base + b, self.blocks.at[self.device(2, b)], self.passing.at[b],
+                             self.device(step, 0))
+        for b in (2, 1, 3, 0):
+            if b in self.PLUS:
+                self.copies.send(self.base + 8 + b, self.blocks.at[self.device(-1, b)],
+                                 self.right.at[b], self.device(-1, 0))
+            else:
+                self.copies.send(self.base + 4 + b, self.blocks.at[self.device(1, b)],
+                                 self.left.at[b], self.device(1, 0))
+
+    def join(self, b):
+        self.copies.arrived(self.base + b, self.passing.at[b])
+        step = 1 if b in self.PLUS else -1
+        mine = self.blocks[self.device(step, b)].astype(jnp.float32)
+        self.joined[b] = (mine + self.passing[b].astype(jnp.float32)).astype(jnp.bfloat16)
+        if step == 1:
+            self.copies.send(self.base + 4 + b, self.joined.at[b], self.left.at[b], self.device(1, 0))
+        else:
+            self.copies.send(self.base + 8 + b, self.joined.at[b], self.right.at[b], self.device(-1, 0))
+
+    def total(self, b):
+        self.copies.arrived(self.base + 4 + b, self.left.at[b])
+        self.copies.arrived(self.base + 8 + b, self.right.at[b])
+        total = (self.blocks[self.device(0, b)].astype(jnp.float32)
+                 + self.left[b].astype(jnp.float32) + self.right[b].astype(jnp.float32))
+        if b == 0:
+            self.own_sum[...] = total
+        else:
+            self.sums[b] = total.astype(jnp.bfloat16)
+
+    def rows(self, half):
+        return pl.ds(half * self.half, self.half)
+
+    def begin2(self, b):
+        if b == 2:
+            for half in (0, 1):
+                self.copies.send(self.base + 12 + half, self.sums.at[2, self.rows(half)],
+                                 self.passing2.at[half], self.device(0, 1 - 2 * half))
+        elif b == 1:
+            self.copies.send(self.base + 14, self.sums.at[1, self.rows(1)],
+                             self.left2.at[self.rows(1)], self.device(0, 1))
+        else:
+            self.copies.send(self.base + 15, self.sums.at[3, self.rows(0)],
+                             self.right2.at[self.rows(0)], self.device(0, -1))
+
+    def join2(self, half):
+        self.copies.arrived(self.base + 12 + half, self.passing2.at[half])
+        b = 1 if half == 0 else 3
+        mine = self.sums[b, self.rows(half)].astype(jnp.float32)
+        self.joined2[half] = (mine + self.passing2[half].astype(jnp.float32)).astype(jnp.bfloat16)
+        if half == 0:
+            self.copies.send(self.base + 16, self.joined2.at[0], self.left2.at[self.rows(0)],
+                             self.device(0, 1))
+        else:
+            self.copies.send(self.base + 17, self.joined2.at[1], self.right2.at[self.rows(1)],
+                             self.device(0, -1))
+
+    def end(self):
+        self.copies.arrived(self.base + 14, self.left2.at[self.rows(1)])
+        self.copies.arrived(self.base + 15, self.right2.at[self.rows(0)])
+        self.copies.arrived(self.base + 16, self.left2.at[self.rows(0)])
+        self.copies.arrived(self.base + 17, self.right2.at[self.rows(1)])
+        total = self.own_sum[...] + self.left2[...].astype(jnp.float32) + self.right2[...].astype(jnp.float32)
+        self.out[...] = total.astype(jnp.bfloat16)
+
+
+def collect_kernel(dk_ref, dv_ref, dk_out, dv_out, passing, joined, left, right, sums, own_sum,
+                   passing2, joined2, left2, right2, send_sems, recv_sems):
+    copies = Copies(send_sems, recv_sems)
+    k_sum, v_sum = [
+        Collect(i == 0, blocks, out, copies, 18 * i, passing.at[i], joined.at[i], left.at[i], right.at[i],
+                sums.at[i], own_sum.at[i], passing2.at[i], joined2.at[i], left2.at[i], right2.at[i])
+        for i, (blocks, out) in enumerate(((dk_ref, dk_out), (dv_ref, dv_out)))]
+    both = (k_sum, v_sum)
+    greet([(1, 0), (3, 0), (0, 1), (0, 3)])
+    for one in both:
+        one.begin()
+    for b in (2, 1, 0, 3):
+        for one in both:
+            one.join(b)
+    for b in (2, 1, 3):
+        for one in both:
+            one.total(b)
+            one.begin2(b)
+    for half in (0, 1):
+        for one in both:
+            one.join2(half)
+    for one in both:
+        one.total(0)
+    for one in both:
+        one.end()
+    copies.finish()
+
+
+def collect(dk, dv):
+    shards, local, width = dk.shape
+    bf16 = jnp.bfloat16
+    vmem = pl.BlockSpec(memory_space=pltpu.VMEM)
+    full = (2, SIDE, local, width)
+    return pl.pallas_call(
+        collect_kernel,
+        out_shape=(jax.ShapeDtypeStruct((local, width), bf16),) * 2,
+        in_specs=[vmem, vmem],
+        out_specs=(vmem, vmem),
+        scratch_shapes=[
+            pltpu.VMEM(full, bf16), pltpu.VMEM(full, bf16), pltpu.VMEM(full, bf16), pltpu.VMEM(full, bf16),
+            pltpu.VMEM(full, bf16), pltpu.VMEM((2, local, width), jnp.float32),
+            pltpu.VMEM((2, 2, local // 2, width), bf16), pltpu.VMEM((2, 2, local // 2, width), bf16),
+            pltpu.VMEM((2, local, width), bf16), pltpu.VMEM((2, local, width), bf16),
+            pltpu.SemaphoreType.DMA((36,)),
+            pltpu.SemaphoreType.DMA((36,)),
+        ],
+        compiler_params=pltpu.CompilerParams(
+            collective_id=1, has_side_effects=True, vmem_limit_bytes=24 << 20),
+    )(dk, dv)
+
+
+def attention_kernel(tile, scale, me, lengths, owners, qg_ref, k_ref, v_ref,
+                     out_ref, dq_ref, dk_ref, dv_ref,
                      kvt, acc, pair, s_buf, d_buf, o_acc, dq_acc):
     if me is None:
         me = lax.axis_index("ctx")
-    shards, rows, width = q_ref.shape
-    keys = kv_ref.shape[0]
+    shards, rows, width = qg_ref.shape
+    rows = rows // 2
+    keys = k_ref.shape[0]
     ndocs = lengths.shape[0]
     shard_rows = keys // shards
     block = shard_rows // shards
@@ -40,8 +355,8 @@
     @pl.loop(0, keys // 128)
     def _(b):
         at = pl.ds(pl.multiple_of(b * 128, 128), 128)
-        kvt[0:width, at] = kv_ref[at, 0:width].T
-        kvt[width:2 * width, at] = kv_ref[at, width:2 * width].T
+        kvt[0:width, at] = k_ref[at, :].T
+        kvt[width:2 * width, at] = v_ref[at, :].T
 
     token = lax.broadcasted_iota(jnp.int32, (1, rows), 1) // heads
     key_index = lax.broadcasted_iota(jnp.int32, (tile, rows), 0)
@@ -50,7 +365,7 @@
     def _(j):
         slot = jnp.int32(0)
         for s in range(shards):
-            slot = slot + jnp.where(owners[j, s] == me, s, 0)
+            slot = jnp.where(owners[j, s] == me, s, slot)
         first = j * shard_rows + slot * block
         pos = first + token
         start = jnp.zeros_like(pos)
@@ -63,8 +378,8 @@
         base = (low // 128) * 128
         count = (first + block - base + tile - 1) // tile
 
-        pair[0:rows, 0:width] = q_ref[j]
-        pair[rows:2 * rows, width:2 * width] = g_ref[j]
+        pair[0:rows, 0:width] = qg_ref[j, 0:rows]
+        pair[rows:2 * rows, width:2 * width] = qg_ref[j, rows:2 * rows]
 
         def window(t):
             want = base + t * tile
@@ -72,7 +387,8 @@
 
         def scores(t, peak):
             want, at = window(t)
-            both = dot(kv_ref[pl.ds(at, tile), :], pair[...], NT)
+            span = pl.ds(at, tile)
+            both = dot(jnp.concatenate([k_ref[span, :], v_ref[span, :]], axis=1), pair[...], NT)
             lower = jnp.maximum(start, want) - at
             allowed = (key_index >= lower) & (key_index <= pos - at)
             s = jnp.where(allowed, both[:, 0:rows], NEG)
@@ -120,26 +436,29 @@
             rows_at = pl.ds(pl.multiple_of(j * shard_rows + s * block, block), block)
             part = acc[rows_at, :]
             owner = owners[j, s]
-            dkv_ref[owner, j, :, 0:width] = (part[:, 0:width] * scale).astype(jnp.bfloat16)
-            dkv_ref[owner, j, :, width:2 * width] = part[:, width:2 * width].astype(jnp.bfloat16)
-
-
-def attention(q, g, kv, lengths, owners, me=None, tile=512, interpret=False):
-    shards, rows, width = q.shape
-    keys = kv.shape[0]
+            dk_ref[owner, j] = (part[:, 0:width] * scale).astype(jnp.bfloat16)
+            dv_ref[owner, j] = part[:, width:2 * width].astype(jnp.bfloat16)
+
+
+def attention(qg, k, v, lengths, owners, me=None, tile=512, interpret=False):
+    shards, rows, width = qg.shape
+    rows = rows // 2
+    local = k.shape[1]
+    keys = shards * local
     block = keys // shards // shards
     reach = -(-(2048 + block + 128) // tile) * tile
     smem = pl.BlockSpec(memory_space=pltpu.SMEM)
     vmem = pl.BlockSpec(memory_space=pltpu.VMEM)
-    return pl.pallas_call(
+    out, dq, dk, dv = pl.pallas_call(
         functools.partial(attention_kernel, tile, width ** -0.5, me),
         out_shape=(
             jax.ShapeDtypeStruct((shards, rows, width), jnp.bfloat16),
             jax.ShapeDtypeStruct((shards, rows, width), jnp.bfloat16),
-            jax.ShapeDtypeStruct((shards, shards, block, 2 * width), jnp.bfloat16),
+            jax.ShapeDtypeStruct((shards, shards, block, width), jnp.bfloat16),
+            jax.ShapeDtypeStruct((shards, shards, block, width), jnp.bfloat16),
         ),
         in_specs=[smem, smem, vmem, vmem, vmem],
-        out_specs=(vmem, vmem, vmem),
+        out_specs=(vmem, vmem, vmem, vmem),
         scratch_shapes=[
             pltpu.VMEM((2 * width, keys), jnp.bfloat16),
             pltpu.VMEM((keys, 2 * width), jnp.float32),
@@ -151,30 +470,23 @@
         ],
         compiler_params=pltpu.CompilerParams(vmem_limit_bytes=40 << 20),
         interpret=interpret,
-    )(lengths, owners, q, g, kv)
+    )(lengths, owners, qg, k.reshape(keys, width), v.reshape(keys, width))
+    return out, dq, dk.reshape(shards, local, width), dv.reshape(shards, local, width)
 
 
 def on_device(query, keys, values, output_gradient, doc_lengths, block_owner):
-    shards = lax.axis_size("ctx")
-    me = lax.axis_index("ctx")
     local, heads, width = query.shape
-    block = local // shards
-    targets = lax.dynamic_index_in_dim(block_owner, me, 0, keepdims=False)
-    ids = jnp.arange(shards, dtype=jnp.int32)
-    order = jnp.sum((targets[:, None] == ids[None, :]).astype(jnp.int32) * ids[:, None], axis=0)
-
-    def arrange(source):
-        moved = jnp.take(source.reshape(shards, block * heads, width), order, axis=0)
-        return lax.all_to_all(moved, "ctx", split_axis=0, concat_axis=0, tiled=True)
-
-    kv = lax.all_gather(jnp.concatenate([keys[:, 0], values[:, 0]], axis=1), "ctx", tiled=True)
-    out, dq, dkv = attention(arrange(query), arrange(output_gradient), kv, doc_lengths, block_owner)
-    dkv = lax.psum_scatter(dkv, "ctx", scatter_dimension=0, tiled=True).reshape(local, 2 * width)
+    shards = SIDE * SIDE
+    rows = local // shards * heads
+    qg, k, v = exchange(block_owner, query.reshape(shards, rows, width),
+                        output_gradient.reshape(shards, rows, width), keys[:, 0], values[:, 0])
+    out, dq, dk, dv = attention(qg, k, v, doc_lengths, block_owner)
+    dk, dv = collect(dk, dv)
     return (
         out.reshape(local, heads, width),
         dq.reshape(local, heads, width),
-        dkv[:, None, :width],
-        dkv[:, None, width:],
+        dk[:, None],
+        dv[:, None],
     )
 
 

time: 175 us -> 84.4 us (0.48)
  waiting for transfers between devices: 90.6 us -> 0 us
  Pallas kernels: 27.9 us -> 76.3 us
  blocking collectives: 33.8 us -> 0 us
  between operations: 14.1 us -> 0.68 us
  other arithmetic: 1.88 us -> 0 us
    unnamed x3 -> x0, waiting for transfers between devices: 76.3 us -> none
    pallas_call x0 -> x2, Pallas kernels: none -> 49.8 us  [the longest x1 31.8 us: exchange(): pl.pallas_call(exchange_kernel, out_shape=(jax.ShapeDtypeStruct((shards,...]
    all_to_all x2 -> x0, blocking collectives: 33.8 us -> none  [arrange(): return lax.all_to_all(moved, 'ctx', split_axis=0, concat_axis=0, tiled=True)]
    all_gather x1 -> x0, waiting for transfers between devices: 14.3 us -> none  [on_device(): lax.all_gather(jnp.concatenate([keys[:, 0], values[:, 0]], axis=1), 'ctx'...]
    unnamed x8 -> x16, local copies, waits for them, and re-layouts: 1.61 us -> 6.4 us
    gather x2 -> x0, local copies, waits for them, and re-layouts: 2.34 us -> none  [arrange(): jnp.take(source.reshape(shards, block * heads, width), order, axis=0)]
  transfers between devices with their start and end apart: 2 -> 0, of which waited for: 2 -> 0; matrix products, arithmetic and copies ran while one was open for 2% -> 0% of each run, Pallas kernels for 0% -> 0%
where the time goes in v2:
time: 84.4 us; the launch traced here: 83.4 us
  Pallas kernels  76.3 us (90%)
  local copies, waits for them, and re-layouts  6.4 us (8%)
    pallas_call x1, Pallas kernels, exchange(): pl.pallas_call(exchange_kernel, out_shape=(jax.ShapeDtypeStruct((shards,...  31.8 us
    pallas_call x1, Pallas kernels, attention(): pl.pallas_call(functools.partial(attention_kernel, tile, width ** (-0.5),...  26.5 us
    pallas_call x1, Pallas kernels, collect(): pl.pallas_call(collect_kernel, out_shape=(jax.ShapeDtypeStruct((local, wi...  18 us
    unnamed x16, local copies, waits for them, and re-layouts  6.4 us

profile of v2, /device:TPU:0, one launch (start us, length us, event | category | flops | bytes accessed | tf_op | source)
XLA Modules:
  0.0 83.4 jit_solution(2036186790345639633)
XLA Ops:
  0.6 0.0 copy-start
  0.6 1.0 %copy-done = bf16[256,8,128]{2,1,0:T(8,128)(2,1)S(1)} copy-done((bf16[256,8,128]{2,1,0:T(8,128)(2,1)S(1)}, bf16[256,8,128]{2,1,0:T(8,128)(2,1)}, u32[]{:S(2)}) %copy-start) | copy-done | bytes 524312
  1.7 0.0 copy-start.1
  1.7 1.0 %copy-done.1 = bf16[256,8,128]{2,1,0:T(8,128)(2,1)S(1)} copy-done((bf16[256,8,128]{2,1,0:T(8,128)(2,1)S(1)}, bf16[256,8,128]{2,1,0:T(8,128)(2,1)}, u32[]{:S(2)}) %copy-start.1) | copy-done | bytes 524312
  2.7 0.0 copy-start.2
  2.7 0.8 %copy-done.2 = bf16[256,1,128]{2,0,1:T(8,128)(2,1)S(1)} copy-done((bf16[256,1,128]{2,0,1:T(8,128)(2,1)S(1)}, bf16[256,1,128]{2,0,1:T(8,128)(2,1)}, u32[]{:S(2)}) %copy-start.2) | copy-done | bytes 65560
  3.6 0.0 copy-start.3
  3.6 0.8 %copy-done.3 = bf16[256,1,128]{2,0,1:T(8,128)(2,1)S(1)} copy-done((bf16[256,1,128]{2,0,1:T(8,128)(2,1)S(1)}, bf16[256,1,128]{2,0,1:T(8,128)(2,1)}, u32[]{:S(2)}) %copy-start.3) | copy-done | bytes 65560
  4.4 0.0 copy-start.4
  4.4 0.7 copy-done.4
  5.1 31.8 %shard_map.93 = (bf16[16,256,128]{2,1,0:T(8,128)(2,1)S(1)}, bf16[16,256,128]{2,1,0:T(8,128)(2,1)S(1)}, bf16[16,256,128]{2,1,0:T(8,128)(2,1)S(1)}) custom-call(s32[16,16]{1,0:T(8,128)S(1)} %copy-done.4, bf16[16,128,128]{2,1,0:T(8,128)(2,1)S(1)} %bitcast.16, bf16[16,128,128]{2,1,0:T(8,128)(2,1)S(1)} %bitcast.17, bf16[256,128]{1,0:T(8,128)(2,1)S(1)} %bitcast.18, ...), custom_call_target="tpu_custom_call" | custom-call | tf_op jit(solution)/shard_map/pallas_call | solution.py:185
  36.9 0.0 copy-start.5
  36.9 0.0 copy-start.6
  36.9 0.7 copy-done.5
  37.6 0.0 copy-done.6
  37.6 26.5 %shard_map.94 = (bf16[16,128,128]{2,1,0:T(8,128)(2,1)}, bf16[16,128,128]{2,1,0:T(8,128)(2,1)}, bf16[16,16,16,128]{3,2,1,0:T(8,128)(2,1)S(1)}, bf16[16,16,16,128]{3,2,1,0:T(8,128)(2,1)S(1)}) custom-call(s32[8]{0:T(128)S(1)} %copy-done.6, s32[16,16]{1,0:T(8,128)S(1)} %copy-done.5, bf16[16,256,128]{2,1,0:T(8,128)(2,1)S(1)} %get-tuple-element.13.qg_ref, ...), custom_call_target="tpu_custom_call" | custom-call | tf_op jit(solution)/shard_map/pallas_call | solution.py:452
  64.1 18.0 %shard_map.95 = (bf16[256,128]{1,0:T(8,128)(2,1)S(1)}, bf16[256,128]{1,0:T(8,128)(2,1)S(1)}) custom-call(bf16[16,256,128]{2,1,0:T(8,128)(2,1)S(1)} %bitcast.12, bf16[16,256,128]{2,1,0:T(8,128)(2,1)S(1)} %bitcast.13), custom_call_target="tpu_custom_call" | custom-call | tf_op jit(solution)/shard_map/pallas_call | solution.py:320
  82.2 0.6 copy.12
  82.8 0.6 copy.13
Async XLA Ops:
  0.6 1.0 %copy-start = (bf16[256,8,128]{2,1,0:T(8,128)(2,1)S(1)}, bf16[256,8,128]{2,1,0:T(8,128)(2,1)}, u32[]{:S(2)}) copy-start(bf16[256,8,128]{2,1,0:T(8,128)(2,1)} %param.6) | copy-start | bytes 1572868
  1.7 1.0 %copy-start.1 = (bf16[256,8,128]{2,1,0:T(8,128)(2,1)S(1)}, bf16[256,8,128]{2,1,0:T(8,128)(2,1)}, u32[]{:S(2)}) copy-start(bf16[256,8,128]{2,1,0:T(8,128)(2,1)} %param.9) | copy-start | bytes 1572868
  2.7 0.8 %copy-start.2 = (bf16[256,1,128]{2,0,1:T(8,128)(2,1)S(1)}, bf16[256,1,128]{2,0,1:T(8,128)(2,1)}, u32[]{:S(2)}) copy-start(bf16[256,1,128]{2,0,1:T(8,128)(2,1)} %param.7) | copy-start | bytes 196612
  3.6 0.8 %copy-start.3 = (bf16[256,1,128]{2,0,1:T(8,128)(2,1)S(1)}, bf16[256,1,128]{2,0,1:T(8,128)(2,1)}, u32[]{:S(2)}) copy-start(bf16[256,1,128]{2,0,1:T(8,128)(2,1)} %param.8) | copy-start | bytes 196612
  4.4 0.7 copy-start.4
  36.9 0.7 copy-start.5
  36.9 0.7 copy-start.6

commit v3 on v2

--- a/solution.py
+++ b/solution.py
@@ -112,20 +112,23 @@
             self.send(2, a, kind, part, part)
 
 
-def exchange_kernel(owners, q_ref, g_ref, k_ref, v_ref, qg_out, k_out, v_out,
-                    staging, send_sems, recv_sems):
+def exchange_kernel(owners, q_hbm, g_hbm, k_hbm, v_hbm, qg_out, k_out, v_out, kvt,
+                    q_in, g_in, staging, load_sems, send_sems, recv_sems):
     me = lax.axis_index(MESH_AXIS)
-    rows = q_ref.shape[1]
+    width = k_out.shape[2]
+    loads = [pltpu.make_async_copy(src, dst, load_sems.at[n]) for n, (src, dst) in enumerate((
+        (k_hbm, k_out.at[me]), (v_hbm, v_out.at[me]), (q_hbm, q_in), (g_hbm, g_in)))]
+    for load in loads:
+        load.start()
     copies = Copies(send_sems, recv_sems)
-    k_spread = Spread(True, k_ref, k_out, copies, 0)
-    v_spread = Spread(False, v_ref, v_out, copies, 20)
-    spreads = (k_spread, v_spread)
-
+    spreads = (Spread(True, k_out.at[me], k_out, copies, 0), Spread(False, v_out.at[me], v_out, copies, 20))
     greet(OFFSETS)
+    loads[0].wait()
+    loads[1].wait()
     for spread in spreads:
         spread.start()
-    k_out[me] = k_ref[...]
-    v_out[me] = v_ref[...]
+    loads[2].wait()
+    loads[3].wait()
 
     def slot_for(target):
         slot = jnp.int32(0)
@@ -137,9 +140,9 @@
         for n in items:
             target = device_at(*OFFSETS[n])
             slot = slot_for(target)
-            staging[n, 0:rows] = q_ref[slot]
-            staging[n, rows:2 * rows] = g_ref[slot]
-            copies.send(40 + n, staging.at[n], qg_out.at[me], target)
+            staging[n, 0] = q_in[slot]
+            staging[n, 1] = g_in[slot]
+            copies.send(40 + n, staging.at[n], qg_out.at[:, me], target)
 
     far = sorted(range(15), key=lambda n: -sum(min(d, SIDE - d) for d in OFFSETS[n]))
     reassign(far[:5])
@@ -159,8 +162,8 @@
             spread.onward(2, 0, kind)
     reassign(far[10:])
     slot = slot_for(me)
-    qg_out[me, 0:rows] = q_ref[slot]
-    qg_out[me, rows:2 * rows] = g_ref[slot]
+    qg_out[0, me] = q_in[slot]
+    qg_out[1, me] = g_in[slot]
     for a in (-1, 1, 2):
         for kind in (0, 1):
             for spread in spreads:
@@ -170,9 +173,17 @@
         for kind in (2, 3):
             for spread in spreads:
                 spread.got(2, a, kind)
+
+    @pl.loop(0, SIDE * SIDE)
+    def _(b):
+        for h in range(k_out.shape[1] // 128):
+            at = pl.ds(pl.multiple_of(b * k_out.shape[1] + h * 128, 128), 128)
+            kvt[0:width, at] = k_out[b, h * 128:(h + 1) * 128].T
+            kvt[width:2 * width, at] = v_out[b, h * 128:(h + 1) * 128].T
+
     for n in far:
         dz, dy = OFFSETS[n]
-        copies.arrived(40 + n, qg_out.at[device_at(-dz, -dy)])
+        copies.arrived(40 + n, qg_out.at[:, device_at(-dz, -dy)])
     copies.finish()
 
 
@@ -181,18 +192,23 @@
     local = k.shape[0]
     smem = pl.BlockSpec(memory_space=pltpu.SMEM)
     vmem = pl.BlockSpec(memory_space=pltpu.VMEM)
+    hbm = pl.BlockSpec(memory_space=pltpu.HBM)
     bf16 = jnp.bfloat16
     return pl.pallas_call(
         exchange_kernel,
         out_shape=(
-            jax.ShapeDtypeStruct((shards, 2 * rows, width), bf16),
+            jax.ShapeDtypeStruct((2, shards, rows, width), bf16),
             jax.ShapeDtypeStruct((shards, local, width), bf16),
             jax.ShapeDtypeStruct((shards, local, width), bf16),
+            jax.ShapeDtypeStruct((2 * width, shards * local), bf16),
         ),
-        in_specs=[smem, vmem, vmem, vmem, vmem],
-        out_specs=(vmem, vmem, vmem),
+        in_specs=[smem, hbm, hbm, hbm, hbm],
+        out_specs=(vmem, vmem, vmem, vmem),
         scratch_shapes=[
-            pltpu.VMEM((shards - 1, 2 * rows, width), bf16),
+            pltpu.VMEM((shards, rows, width), bf16),
+            pltpu.VMEM((shards, rows, width), bf16),
+            pltpu.VMEM((shards - 1, 2, rows, width), bf16),
+            pltpu.SemaphoreType.DMA((4,)),
             pltpu.SemaphoreType.DMA((55,)),
             pltpu.SemaphoreType.DMA((55,)),
         ],
@@ -335,142 +351,149 @@
     )(dk, dv)
 
 
-def attention_kernel(tile, scale, me, lengths, owners, qg_ref, k_ref, v_ref,
-                     out_ref, dq_ref, dk_ref, dv_ref,
-                     kvt, acc, pair, s_buf, d_buf, o_acc, dq_acc):
+SIZES = (512, 768, 1024, 1536, 2048, 2816)
+CHUNK = 256
+
+
+def attention_kernel(scale, me, lengths, owners, qg_ref, k_ref, v_ref, kvt,
+                     out_hbm, dq_hbm, dk_ref, dv_ref,
+                     dk_acc, dv_acc, s_buf, p_buf, sl_buf, out_buf, dq_buf, sems):
     if me is None:
         me = lax.axis_index("ctx")
-    shards, rows, width = qg_ref.shape
-    rows = rows // 2
+    _, pairs, rows, width = qg_ref.shape
+    shards = 2 * pairs
     keys = k_ref.shape[0]
     ndocs = lengths.shape[0]
     shard_rows = keys // shards
     block = shard_rows // shards
-    heads = rows // block
+    half = rows // 2
+    heads = half // block
     per_scale = scale * LOG2E
-
-    acc[...] = jnp.zeros_like(acc)
-    pair[...] = jnp.zeros_like(pair)
-
-    @pl.loop(0, keys // 128)
-    def _(b):
-        at = pl.ds(pl.multiple_of(b * 128, 128), 128)
-        kvt[0:width, at] = k_ref[at, :].T
-        kvt[width:2 * width, at] = v_ref[at, :].T
-
-    token = lax.broadcasted_iota(jnp.int32, (1, rows), 1) // heads
-    key_index = lax.broadcasted_iota(jnp.int32, (tile, rows), 0)
-
-    @pl.loop(0, shards)
-    def _(j):
-        slot = jnp.int32(0)
-        for s in range(shards):
-            slot = jnp.where(owners[j, s] == me, s, slot)
-        first = j * shard_rows + slot * block
-        pos = first + token
+    f32, bf16 = jnp.float32, jnp.bfloat16
+
+    dk_acc[...] = jnp.zeros_like(dk_acc)
+    dv_acc[...] = jnp.zeros_like(dv_acc)
+    lane = lax.broadcasted_iota(jnp.int32, (1, rows), 1)
+    second = lane >= half
+    token = jnp.where(second, lane - half, lane) // heads
+    key_index = lax.broadcasted_iota(jnp.int32, (CHUNK, rows), 0)
+
+    def copies(n):
+        return (pltpu.make_async_copy(out_buf.at[n], out_hbm.at[n], sems.at[0, n]),
+                pltpu.make_async_copy(dq_buf.at[n], dq_hbm.at[n], sems.at[1, n]))
+
+    @pl.loop(0, pairs)
+    def _(n):
+        firsts = []
+        for m in range(2):
+            slot = jnp.int32(0)
+            for s in range(shards):
+                slot = jnp.where(owners[2 * n + m, s] == me, s, slot)
+            firsts.append((2 * n + m) * shard_rows + slot * block)
+        pos = jnp.where(second, firsts[1], firsts[0]) + token
         start = jnp.zeros_like(pos)
         low = jnp.int32(0)
         end = jnp.int32(0)
         for d in range(ndocs):
             end = end + lengths[d]
             start = jnp.where(end <= pos, end, start)
-            low = jnp.where(end <= first, end, low)
+            low = jnp.where(end <= firsts[0], end, low)
         base = (low // 128) * 128
-        count = (first + block - base + tile - 1) // tile
-
-        pair[0:rows, 0:width] = qg_ref[j, 0:rows]
-        pair[rows:2 * rows, width:2 * width] = qg_ref[j, rows:2 * rows]
-
-        def window(t):
-            want = base + t * tile
-            return want, pl.multiple_of(jnp.minimum(want, keys - tile), 128)
-
-        def scores(t, peak):
-            want, at = window(t)
-            span = pl.ds(at, tile)
-            both = dot(jnp.concatenate([k_ref[span, :], v_ref[span, :]], axis=1), pair[...], NT)
-            lower = jnp.maximum(start, want) - at
-            allowed = (key_index >= lower) & (key_index <= pos - at)
-            s = jnp.where(allowed, both[:, 0:rows], NEG)
-            here = pl.ds(pl.multiple_of(t * tile, tile), tile)
-            s_buf[here, :] = s
-            d_buf[here, :] = both[:, rows:2 * rows]
-            return jnp.maximum(peak, folded(s, jnp.max))
-
-        peak = lax.fori_loop(0, count, scores, jnp.full((8, rows), NEG, jnp.float32))
-        peak = jnp.max(peak, axis=0, keepdims=True)
-
-        def weights(t, sums):
-            here = pl.ds(pl.multiple_of(t * tile, tile), tile)
-            p = jnp.exp2((s_buf[here, :] - peak) * per_scale)
-            s_buf[here, :] = p
-            return sums[0] + folded(p, jnp.sum), sums[1] + folded(p * d_buf[here, :], jnp.sum)
-
-        zero = jnp.zeros((8, rows), jnp.float32)
-        total, delta = lax.fori_loop(0, count, weights, (zero, zero))
-        inverse = 1.0 / jnp.sum(total, axis=0, keepdims=True)
-        delta = jnp.sum(delta, axis=0, keepdims=True) * inverse
-
-        o_acc[...] = jnp.zeros_like(o_acc)
-        dq_acc[...] = jnp.zeros_like(dq_acc)
-
-        @pl.loop(0, count)
-        def _(t):
-            _, at = window(t)
-            here = pl.ds(pl.multiple_of(t * tile, tile), tile)
-            probs = s_buf[here, :] * inverse
-            slopes = probs * (d_buf[here, :] - delta)
-            probs = probs.astype(jnp.bfloat16)
-            slopes = slopes.astype(jnp.bfloat16)
-            span = pl.ds(at, tile)
-            acc[span, :] += dot(jnp.concatenate([slopes, probs], axis=1), pair[...], NN)
-            dq_acc[...] += dot(kvt[0:width, span], slopes, NN)
-            o_acc[...] += dot(kvt[width:2 * width, span], probs, NN)
-
-        out_ref[j] = o_acc[...].T.astype(jnp.bfloat16)
-        dq_ref[j] = (dq_acc[...] * scale).T.astype(jnp.bfloat16)
+        need = firsts[1] + block - base
+
+        def work(size):
+            at = pl.multiple_of(jnp.minimum(base, keys - size), 128)
+            lower = start - at
+            upper = pos - at
+            peak = jnp.full((8, rows), NEG, f32)
+            for c in range(size // CHUNK):
+                here = slice(c * CHUNK, (c + 1) * CHUNK)
+                raw = dot(k_ref[pl.ds(at + c * CHUNK, CHUNK), :], qg_ref[0, n], NT)
+                allowed = (key_index >= lower - c * CHUNK) & (key_index <= upper - c * CHUNK)
+                x = jnp.where(allowed, raw, NEG)
+                s_buf[here, :] = x
+                peak = jnp.maximum(peak, folded(x, jnp.max))
+            peak = jnp.max(peak, axis=0, keepdims=True)
+            total = jnp.zeros((8, rows), f32)
+            for c in range(size // CHUNK):
+                here = slice(c * CHUNK, (c + 1) * CHUNK)
+                p = jnp.exp2((s_buf[here, :] - peak) * per_scale)
+                p_buf[here, :] = p.astype(bf16)
+                total = total + folded(p, jnp.sum)
+            inverse = 1.0 / jnp.sum(total, axis=0, keepdims=True)
+            span = pl.ds(at, size)
+            out = dot(kvt[width:2 * width, span], p_buf[0:size, :], NN)
+            out = (out * inverse).T.astype(bf16)
+            out_buf[n] = out
+            delta = jnp.sum((out.astype(f32) * qg_ref[1, n].astype(f32)).T, axis=0, keepdims=True)
+            for c in range(size // CHUNK):
+                here = slice(c * CHUNK, (c + 1) * CHUNK)
+                spot = pl.ds(at + c * CHUNK, CHUNK)
+                products = dot(v_ref[spot, :], qg_ref[1, n], NT)
+                probs = p_buf[here, :].astype(f32) * inverse
+                slopes = (probs * (products - delta)).astype(bf16)
+                sl_buf[here, :] = slopes
+                dk_acc[spot, :] += dot(slopes, qg_ref[0, n], NN)
+                dv_acc[spot, :] += dot(probs.astype(bf16), qg_ref[1, n], NN)
+            dq = dot(kvt[0:width, span], sl_buf[0:size, :], NN)
+            dq_buf[n] = (dq * scale).T.astype(bf16)
+
+        for small, size in zip((0,) + SIZES, SIZES):
+            @pl.when((need > small) & (need <= size))
+            def _():
+                work(size)
+
+        for copy in copies(n):
+            copy.start()
 
     @pl.loop(0, shards)
     def _(j):
         for s in range(shards):
             rows_at = pl.ds(pl.multiple_of(j * shard_rows + s * block, block), block)
-            part = acc[rows_at, :]
             owner = owners[j, s]
-            dk_ref[owner, j] = (part[:, 0:width] * scale).astype(jnp.bfloat16)
-            dv_ref[owner, j] = part[:, width:2 * width].astype(jnp.bfloat16)
-
-
-def attention(qg, k, v, lengths, owners, me=None, tile=512, interpret=False):
-    shards, rows, width = qg.shape
-    rows = rows // 2
+            dk_ref[owner, j] = (dk_acc[rows_at, :] * scale).astype(bf16)
+            dv_ref[owner, j] = dv_acc[rows_at, :].astype(bf16)
+
+    @pl.loop(0, pairs)
+    def _(n):
+        for copy in copies(n):
+            copy.wait()
+
+
+def attention(qg, k, v, kvt, lengths, owners, me=None, interpret=False):
+    _, shards, half, width = qg.shape
+    rows = 2 * half
+    pairs = shards // 2
     local = k.shape[1]
     keys = shards * local
-    block = keys // shards // shards
-    reach = -(-(2048 + block + 128) // tile) * tile
+    block = local // shards
     smem = pl.BlockSpec(memory_space=pltpu.SMEM)
     vmem = pl.BlockSpec(memory_space=pltpu.VMEM)
+    hbm = pl.BlockSpec(memory_space=pltpu.HBM)
+    f32, bf16 = jnp.float32, jnp.bfloat16
     out, dq, dk, dv = pl.pallas_call(
-        functools.partial(attention_kernel, tile, width ** -0.5, me),
+        functools.partial(attention_kernel, width ** -0.5, me),
         out_shape=(
-            jax.ShapeDtypeStruct((shards, rows, width), jnp.bfloat16),
-            jax.ShapeDtypeStruct((shards, rows, width), jnp.bfloat16),
-            jax.ShapeDtypeStruct((shards, shards, block, width), jnp.bfloat16),
-            jax.ShapeDtypeStruct((shards, shards, block, width), jnp.bfloat16),
+            jax.ShapeDtypeStruct((pairs, rows, width), bf16),
+            jax.ShapeDtypeStruct((pairs, rows, width), bf16),
+            jax.ShapeDtypeStruct((shards, shards, block, width), bf16),
+            jax.ShapeDtypeStruct((shards, shards, block, width), bf16),
         ),
-        in_specs=[smem, smem, vmem, vmem, vmem],
-        out_specs=(vmem, vmem, vmem, vmem),
+        in_specs=[smem, smem, vmem, vmem, vmem, vmem],
+        out_specs=(hbm, hbm, vmem, vmem),
         scratch_shapes=[
-            pltpu.VMEM((2 * width, keys), jnp.bfloat16),
-            pltpu.VMEM((keys, 2 * width), jnp.float32),
-            pltpu.VMEM((2 * rows, 2 * width), jnp.bfloat16),
-            pltpu.VMEM((reach, rows), jnp.float32),
-            pltpu.VMEM((reach, rows), jnp.float32),
-            pltpu.VMEM((width, rows), jnp.float32),
-            pltpu.VMEM((width, rows), jnp.float32),
+            pltpu.VMEM((keys, width), f32),
+            pltpu.VMEM((keys, width), f32),
+            pltpu.VMEM((SIZES[-1], rows), f32),
+            pltpu.VMEM((SIZES[-1], rows), bf16),
+            pltpu.VMEM((SIZES[-1], rows), bf16),
+            pltpu.VMEM((pairs, rows, width), bf16),
+            pltpu.VMEM((pairs, rows, width), bf16),
+            pltpu.SemaphoreType.DMA((2, pairs)),
         ],
         compiler_params=pltpu.CompilerParams(vmem_limit_bytes=40 << 20),
         interpret=interpret,
-    )(lengths, owners, qg, k.reshape(keys, width), v.reshape(keys, width))
+    )(lengths, owners, qg.reshape(2, pairs, rows, width), k.reshape(keys, width), v.reshape(keys, width), kvt)
     return out, dq, dk.reshape(shards, local, width), dv.reshape(shards, local, width)
 
 
@@ -478,9 +501,9 @@
     local, heads, width = query.shape
     shards = SIDE * SIDE
     rows = local // shards * heads
-    qg, k, v = exchange(block_owner, query.reshape(shards, rows, width),
-                        output_gradient.reshape(shards, rows, width), keys[:, 0], values[:, 0])
-    out, dq, dk, dv = attention(qg, k, v, doc_lengths, block_owner)
+    qg, k, v, kvt = exchange(block_owner, query.reshape(shards, rows, width),
+                             output_gradient.reshape(shards, rows, width), keys[:, 0], values[:, 0])
+    out, dq, dk, dv = attention(qg, k, v, kvt, doc_lengths, block_owner)
     dk, dv = collect(dk, dv)
     return (
         out.reshape(local, heads, width),

time: 84.4 us -> 78.6 us (0.931)
  Pallas kernels: 76.3 us -> 70.2 us
    pallas_call x2, Pallas kernels: 58.3 us -> 51.4 us  [the longest x1 33.6 us: exchange(): pl.pallas_call(exchange_kernel, out_shape=(jax.ShapeDtypeStruct((2, shard...]
where the time goes in v3:
time: 78.6 us; the launch traced here: 77.9 us
  Pallas kernels  70.2 us (89%)
  local copies, waits for them, and re-layouts  7.06 us (9%)
    pallas_call x1, Pallas kernels, exchange(): pl.pallas_call(exchange_kernel, out_shape=(jax.ShapeDtypeStruct((2, shard...  33.6 us
    pallas_call x1, Pallas kernels, collect(): pl.pallas_call(collect_kernel, out_shape=(jax.ShapeDtypeStruct((local, wi...  18.8 us
    pallas_call x1, Pallas kernels, attention(): pl.pallas_call(functools.partial(attention_kernel, width ** (-0.5), me),...  17.8 us
    unnamed x16, local copies, waits for them, and re-layouts  7.06 us

profile of v3, /device:TPU:0, one launch (start us, length us, event | category | flops | bytes accessed | tf_op | source)
XLA Modules:
  0.0 77.9 jit_solution(14460275270204503130)
XLA Ops:
  0.6 0.0 copy-start
  0.6 1.0 %copy-done = bf16[256,8,128]{2,1,0:T(8,128)(2,1)S(1)} copy-done((bf16[256,8,128]{2,1,0:T(8,128)(2,1)S(1)}, bf16[256,8,128]{2,1,0:T(8,128)(2,1)}, u32[]{:S(2)}) %copy-start) | copy-done | bytes 524312
  1.7 0.0 copy-start.1
  1.7 1.0 %copy-done.1 = bf16[256,8,128]{2,1,0:T(8,128)(2,1)S(1)} copy-done((bf16[256,8,128]{2,1,0:T(8,128)(2,1)S(1)}, bf16[256,8,128]{2,1,0:T(8,128)(2,1)}, u32[]{:S(2)}) %copy-start.1) | copy-done | bytes 524312
  2.7 0.0 copy-start.2
  2.7 0.8 %copy-done.2 = bf16[256,1,128]{2,0,1:T(8,128)(2,1)S(1)} copy-done((bf16[256,1,128]{2,0,1:T(8,128)(2,1)S(1)}, bf16[256,1,128]{2,0,1:T(8,128)(2,1)}, u32[]{:S(2)}) %copy-start.2) | copy-done | bytes 65560
  3.6 0.0 copy-start.3
  3.6 0.8 %copy-done.3 = bf16[256,1,128]{2,0,1:T(8,128)(2,1)S(1)} copy-done((bf16[256,1,128]{2,0,1:T(8,128)(2,1)S(1)}, bf16[256,1,128]{2,0,1:T(8,128)(2,1)}, u32[]{:S(2)}) %copy-start.3) | copy-done | bytes 65560
  4.4 0.0 copy-start.4
  4.4 0.7 copy-done.4
  5.1 33.6 %shard_map.93 = (bf16[2,16,128,128]{3,2,1,0:T(8,128)(2,1)S(1)}, bf16[16,256,128]{2,1,0:T(8,128)(2,1)S(1)}, bf16[16,256,128]{2,1,0:T(8,128)(2,1)S(1)}, bf16[256,4096]{1,0:T(8,128)(2,1)S(1)}) custom-call(s32[16,16]{1,0:T(8,128)S(1)} %copy-done.4, bf16[16,128,128]{2,1,0:T(8,128)(2,1)S(1)} %bitcast.18, bf16[16,128,128]{2,1,0:T(8,128)(2,1)S(1)} %bitcast.19, ...), custom_call_target="tpu_custom_call" | custom-call | tf_op jit(solution)/shard_map/pallas_call | solution.py:197
  38.7 0.0 copy-start.5
  38.7 0.7 copy-done.5
  39.4 0.0 copy-start.6
  39.4 0.7 copy-done.6
  40.0 17.8 %shard_map.94 = (bf16[8,256,128]{2,1,0:T(8,128)(2,1)}, bf16[8,256,128]{2,1,0:T(8,128)(2,1)}, bf16[16,16,16,128]{3,2,1,0:T(8,128)(2,1)S(1)}, bf16[16,16,16,128]{3,2,1,0:T(8,128)(2,1)S(1)}) custom-call(s32[8]{0:T(128)S(1)} %copy-done.6, s32[16,16]{1,0:T(8,128)S(1)} %copy-done.5, bf16[2,8,256,128]{3,2,1,0:T(8,128)(2,1)S(1)} %bitcast.15, ...), custom_call_target="tpu_custom_call" | custom-call | tf_op jit(solution)/shard_map/pallas_call | solution.py:474
  57.8 18.8 %shard_map.95 = (bf16[256,128]{1,0:T(8,128)(2,1)S(1)}, bf16[256,128]{1,0:T(8,128)(2,1)S(1)}) custom-call(bf16[16,256,128]{2,1,0:T(8,128)(2,1)S(1)} %bitcast.13, bf16[16,256,128]{2,1,0:T(8,128)(2,1)S(1)} %bitcast.14), custom_call_target="tpu_custom_call" | custom-call | tf_op jit(solution)/shard_map/pallas_call | solution.py:336
  76.6 0.6 copy.12
  77.3 0.6 copy.13
Async XLA Ops:
  0.6 1.0 %copy-start = (bf16[256,8,128]{2,1,0:T(8,128)(2,1)S(1)}, bf16[256,8,128]{2,1,0:T(8,128)(2,1)}, u32[]{:S(2)}) copy-start(bf16[256,8,128]{2,1,0:T(8,128)(2,1)} %param.6) | copy-start | bytes 1572868
  1.7 1.0 %copy-start.1 = (bf16[256,8,128]{2,1,0:T(8,128)(2,1)S(1)}, bf16[256,8,128]{2,1,0:T(8,128)(2,1)}, u32[]{:S(2)}) copy-start(bf16[256,8,128]{2,1,0:T(8,128)(2,1)} %param.9) | copy-start | bytes 1572868
  2.7 0.8 %copy-start.2 = (bf16[256,1,128]{2,0,1:T(8,128)(2,1)S(1)}, bf16[256,1,128]{2,0,1:T(8,128)(2,1)}, u32[]{:S(2)}) copy-start(bf16[256,1,128]{2,0,1:T(8,128)(2,1)} %param.7) | copy-start | bytes 196612
  3.6 0.8 %copy-start.3 = (bf16[256,1,128]{2,0,1:T(8,128)(2,1)S(1)}, bf16[256,1,128]{2,0,1:T(8,128)(2,1)}, u32[]{:S(2)}) copy-start(bf16[256,1,128]{2,0,1:T(8,128)(2,1)} %param.8) | copy-start | bytes 196612
  4.4 0.7 copy-start.4
  38.7 0.7 copy-start.5
  39.4 0.7 copy-start.6

commit v4 on v3

--- a/solution.py
+++ b/solution.py
@@ -351,100 +351,151 @@
     )(dk, dv)
 
 
-SIZES = (512, 768, 1024, 1536, 2048, 2816)
+SIZES = (256, 512, 768, 1024, 1536, 2304)
 CHUNK = 256
 
 
 def attention_kernel(scale, me, lengths, owners, qg_ref, k_ref, v_ref, kvt,
                      out_hbm, dq_hbm, dk_ref, dv_ref,
-                     dk_acc, dv_acc, s_buf, p_buf, sl_buf, out_buf, dq_buf, sems):
+                     dk_acc, dv_acc, out_buf, dq_buf, sems, *lanes):
     if me is None:
         me = lax.axis_index("ctx")
-    _, pairs, rows, width = qg_ref.shape
-    shards = 2 * pairs
+    _, shards, rows, width = qg_ref.shape
     keys = k_ref.shape[0]
     ndocs = lengths.shape[0]
     shard_rows = keys // shards
     block = shard_rows // shards
-    half = rows // 2
-    heads = half // block
+    heads = rows // block
     per_scale = scale * LOG2E
     f32, bf16 = jnp.float32, jnp.bfloat16
+    together = len(lanes) // 3
+    lanes = [lanes[3 * n:3 * n + 3] for n in range(together)]
 
     dk_acc[...] = jnp.zeros_like(dk_acc)
     dv_acc[...] = jnp.zeros_like(dv_acc)
-    lane = lax.broadcasted_iota(jnp.int32, (1, rows), 1)
-    second = lane >= half
-    token = jnp.where(second, lane - half, lane) // heads
+    token = lax.broadcasted_iota(jnp.int32, (1, rows), 1) // heads
     key_index = lax.broadcasted_iota(jnp.int32, (CHUNK, rows), 0)
 
-    def copies(n):
-        return (pltpu.make_async_copy(out_buf.at[n], out_hbm.at[n], sems.at[0, n]),
-                pltpu.make_async_copy(dq_buf.at[n], dq_hbm.at[n], sems.at[1, n]))
-
-    @pl.loop(0, pairs)
-    def _(n):
-        firsts = []
-        for m in range(2):
+    def copies(j):
+        return (pltpu.make_async_copy(out_buf.at[j], out_hbm.at[j], sems.at[0, j]),
+                pltpu.make_async_copy(dq_buf.at[j], dq_hbm.at[j], sems.at[1, j]))
+
+    class Segment:
+        def __init__(self, j, lane):
+            self.j = j
+            self.q, self.g = qg_ref.at[0, j], qg_ref.at[1, j]
+            self.s_buf, self.d_buf, self.sp_buf = lanes[lane]
             slot = jnp.int32(0)
             for s in range(shards):
-                slot = jnp.where(owners[2 * n + m, s] == me, s, slot)
-            firsts.append((2 * n + m) * shard_rows + slot * block)
-        pos = jnp.where(second, firsts[1], firsts[0]) + token
-        start = jnp.zeros_like(pos)
-        low = jnp.int32(0)
-        end = jnp.int32(0)
-        for d in range(ndocs):
-            end = end + lengths[d]
-            start = jnp.where(end <= pos, end, start)
-            low = jnp.where(end <= firsts[0], end, low)
-        base = (low // 128) * 128
-        need = firsts[1] + block - base
-
-        def work(size):
-            at = pl.multiple_of(jnp.minimum(base, keys - size), 128)
-            lower = start - at
-            upper = pos - at
-            peak = jnp.full((8, rows), NEG, f32)
-            for c in range(size // CHUNK):
-                here = slice(c * CHUNK, (c + 1) * CHUNK)
-                raw = dot(k_ref[pl.ds(at + c * CHUNK, CHUNK), :], qg_ref[0, n], NT)
-                allowed = (key_index >= lower - c * CHUNK) & (key_index <= upper - c * CHUNK)
-                x = jnp.where(allowed, raw, NEG)
-                s_buf[here, :] = x
-                peak = jnp.maximum(peak, folded(x, jnp.max))
-            peak = jnp.max(peak, axis=0, keepdims=True)
-            total = jnp.zeros((8, rows), f32)
-            for c in range(size // CHUNK):
-                here = slice(c * CHUNK, (c + 1) * CHUNK)
-                p = jnp.exp2((s_buf[here, :] - peak) * per_scale)
-                p_buf[here, :] = p.astype(bf16)
-                total = total + folded(p, jnp.sum)
-            inverse = 1.0 / jnp.sum(total, axis=0, keepdims=True)
-            span = pl.ds(at, size)
-            out = dot(kvt[width:2 * width, span], p_buf[0:size, :], NN)
-            out = (out * inverse).T.astype(bf16)
-            out_buf[n] = out
-            delta = jnp.sum((out.astype(f32) * qg_ref[1, n].astype(f32)).T, axis=0, keepdims=True)
-            for c in range(size // CHUNK):
-                here = slice(c * CHUNK, (c + 1) * CHUNK)
-                spot = pl.ds(at + c * CHUNK, CHUNK)
-                products = dot(v_ref[spot, :], qg_ref[1, n], NT)
-                probs = p_buf[here, :].astype(f32) * inverse
-                slopes = (probs * (products - delta)).astype(bf16)
-                sl_buf[here, :] = slopes
-                dk_acc[spot, :] += dot(slopes, qg_ref[0, n], NN)
-                dv_acc[spot, :] += dot(probs.astype(bf16), qg_ref[1, n], NN)
-            dq = dot(kvt[0:width, span], sl_buf[0:size, :], NN)
-            dq_buf[n] = (dq * scale).T.astype(bf16)
-
+                slot = jnp.where(owners[j, s] == me, s, slot)
+            first = j * shard_rows + slot * block
+            self.pos = first + token
+            start = jnp.zeros_like(self.pos)
+            low = jnp.int32(0)
+            end = jnp.int32(0)
+            for d in range(ndocs):
+                end = end + lengths[d]
+                start = jnp.where(end <= self.pos, end, start)
+                low = jnp.where(end <= first, end, low)
+            self.start = start
+            self.base = (low // 128) * 128
+            self.need = first + block - self.base
+
+        def open(self, size):
+            self.size = size
+            self.at = pl.multiple_of(jnp.minimum(self.base, keys - size), 128)
+            self.lower = self.start - self.at
+            self.upper = self.pos - self.at
+            self.peak = jnp.full((8, rows), NEG, f32)
+            self.total = jnp.zeros((8, rows), f32)
+            self.dsum = jnp.zeros((8, rows), f32)
+
+        def scores(self, c):
+            here = slice(c * CHUNK, (c + 1) * CHUNK)
+            span = pl.ds(self.at + c * CHUNK, CHUNK)
+            raw = dot(k_ref[span, :], self.q[...], NT)
+            self.d_buf[here, :] = dot(v_ref[span, :], self.g[...], NT)
+            allowed = (key_index >= self.lower - c * CHUNK) & (key_index <= self.upper - c * CHUNK)
+            x = jnp.where(allowed, raw, NEG)
+            self.s_buf[here, :] = x
+            self.peak = jnp.maximum(self.peak, folded(x, jnp.max))
+
+        def peaked(self):
+            self.peak = jnp.max(self.peak, axis=0, keepdims=True)
+
+        def weights(self, c):
+            here = slice(c * CHUNK, (c + 1) * CHUNK)
+            p = jnp.exp2((self.s_buf[here, :] - self.peak) * per_scale)
+            self.s_buf[here, :] = p
+            self.total = self.total + folded(p, jnp.sum)
+            self.dsum = self.dsum + folded(p * self.d_buf[here, :], jnp.sum)
+
+        def summed(self):
+            self.inverse = 1.0 / jnp.sum(self.total, axis=0, keepdims=True)
+            self.delta = jnp.sum(self.dsum, axis=0, keepdims=True) * self.inverse
+
+        def slopes(self, c):
+            here = slice(c * CHUNK, (c + 1) * CHUNK)
+            probs = self.s_buf[here, :] * self.inverse
+            slopes = probs * (self.d_buf[here, :] - self.delta)
+            slopes, probs = slopes.astype(bf16), probs.astype(bf16)
+            self.sp_buf[here, 0:rows] = slopes
+            self.sp_buf[here, rows:2 * rows] = probs
+            spot = pl.ds(self.at + c * CHUNK, CHUNK)
+            dk_acc[spot, :] += dot(slopes, self.q[...], NN)
+            dv_acc[spot, :] += dot(probs, self.g[...], NN)
+
+        def finish(self):
+            span = pl.ds(self.at, self.size)
+            here = slice(0, self.size)
+            dq = dot(kvt[0:width, span], self.sp_buf[here, 0:rows], NN)
+            out = dot(kvt[width:2 * width, span], self.sp_buf[here, rows:2 * rows], NN)
+            dq_buf[self.j] = (dq * scale).T.astype(bf16)
+            out_buf[self.j] = out.T.astype(bf16)
+
+    def work(segments, size):
+        chunks = range(size // CHUNK)
+        for one in segments:
+            one.open(size)
+        for c in chunks:
+            segments[0].scores(c)
+        segments[0].peaked()
+        if len(segments) == 1:
+            for c in chunks:
+                segments[0].weights(c)
+            segments[0].summed()
+            for c in chunks:
+                segments[0].slopes(c)
+            segments[0].finish()
+            return
+        for c in chunks:
+            segments[0].weights(c)
+            segments[1].scores(c)
+        segments[0].summed()
+        segments[1].peaked()
+        for c in chunks:
+            segments[0].slopes(c)
+            segments[1].weights(c)
+        segments[1].summed()
+        segments[0].finish()
+        for c in chunks:
+            segments[1].slopes(c)
+        segments[1].finish()
+
+    @pl.loop(0, shards // together)
+    def _(n):
+        segments = [Segment(n * together + m, m) for m in range(together)]
+        need = segments[0].need
+        for one in segments[1:]:
+            need = jnp.maximum(need, one.need)
         for small, size in zip((0,) + SIZES, SIZES):
             @pl.when((need > small) & (need <= size))
             def _():
-                work(size)
-
-        for copy in copies(n):
-            copy.start()
+                work(segments, size)
+
+        for one in segments:
+            for copy in copies(one.j):
+                copy.start()
 
     @pl.loop(0, shards)
     def _(j):
@@ -454,19 +505,17 @@
             dk_ref[owner, j] = (dk_acc[rows_at, :] * scale).astype(bf16)
             dv_ref[owner, j] = dv_acc[rows_at, :].astype(bf16)
 
-    @pl.loop(0, pairs)
-    def _(n):
-        for copy in copies(n):
+    @pl.loop(0, shards)
+    def _(j):
+        for copy in copies(j):
             copy.wait()
 
 
 def attention(qg, k, v, kvt, lengths, owners, me=None, interpret=False):
-    _, shards, half, width = qg.shape
-    rows = 2 * half
-    pairs = shards // 2
+    _, shards, rows, width = qg.shape
     local = k.shape[1]
     keys = shards * local
-    block = local // shards
+    block = keys // shards // shards
     smem = pl.BlockSpec(memory_space=pltpu.SMEM)
     vmem = pl.BlockSpec(memory_space=pltpu.VMEM)
     hbm = pl.BlockSpec(memory_space=pltpu.HBM)
@@ -474,8 +523,8 @@
     out, dq, dk, dv = pl.pallas_call(
         functools.partial(attention_kernel, width ** -0.5, me),
         out_shape=(
-            jax.ShapeDtypeStruct((pairs, rows, width), bf16),
-            jax.ShapeDtypeStruct((pairs, rows, width), bf16),
+            jax.ShapeDtypeStruct((shards, rows, width), bf16),
+            jax.ShapeDtypeStruct((shards, rows, width), bf16),
             jax.ShapeDtypeStruct((shards, shards, block, width), bf16),
             jax.ShapeDtypeStruct((shards, shards, block, width), bf16),
         ),
@@ -484,16 +533,17 @@
         scratch_shapes=[
             pltpu.VMEM((keys, width), f32),
             pltpu.VMEM((keys, width), f32),
+            pltpu.VMEM((shards, rows, width), bf16),
+            pltpu.VMEM((shards, rows, width), bf16),
+            pltpu.SemaphoreType.DMA((2, shards)),
+        ] + 2 * [
             pltpu.VMEM((SIZES[-1], rows), f32),
-            pltpu.VMEM((SIZES[-1], rows), bf16),
-            pltpu.VMEM((SIZES[-1], rows), bf16),
-            pltpu.VMEM((pairs, rows, width), bf16),
-            pltpu.VMEM((pairs, rows, width), bf16),
-            pltpu.SemaphoreType.DMA((2, pairs)),
+            pltpu.VMEM((SIZES[-1], rows), f32),
+            pltpu.VMEM((SIZES[-1], 2 * rows), bf16),
         ],
         compiler_params=pltpu.CompilerParams(vmem_limit_bytes=40 << 20),
         interpret=interpret,
-    )(lengths, owners, qg.reshape(2, pairs, rows, width), k.reshape(keys, width), v.reshape(keys, width), kvt)
+    )(lengths, owners, qg, k.reshape(keys, width), v.reshape(keys, width), kvt)
     return out, dq, dk.reshape(shards, local, width), dv.reshape(shards, local, width)
 
 

time: 78.6 us -> 77.9 us (level)
    pallas_call x1, Pallas kernels: 17.8 us -> 14.3 us  [attention(): pl.pallas_call(functools.partial(attention_kernel, width ** (-0.5), me),...]
    pallas_call x1, Pallas kernels: 18.8 us -> 21.9 us  [collect(): pl.pallas_call(collect_kernel, out_shape=(jax.ShapeDtypeStruct((local, wi...]
where the time goes in v4:
time: 77.9 us; the launch traced here: 77.5 us
  Pallas kernels  69.8 us (90%)
  local copies, waits for them, and re-layouts  7.06 us (9%)
    pallas_call x1, Pallas kernels, exchange(): pl.pallas_call(exchange_kernel, out_shape=(jax.ShapeDtypeStruct((2, shard...  33.6 us
    pallas_call x1, Pallas kernels, collect(): pl.pallas_call(collect_kernel, out_shape=(jax.ShapeDtypeStruct((local, wi...  21.9 us
    pallas_call x1, Pallas kernels, attention(): pl.pallas_call(functools.partial(attention_kernel, width ** (-0.5), me),...  14.3 us
    unnamed x16, local copies, waits for them, and re-layouts  7.06 us

profile of v4, /device:TPU:0, one launch (start us, length us, event | category | flops | bytes accessed | tf_op | source)
XLA Modules:
  0.0 77.5 jit_solution(343927611381378887)
XLA Ops:
  0.6 0.0 copy-start
  0.6 1.0 %copy-done = bf16[256,8,128]{2,1,0:T(8,128)(2,1)S(1)} copy-done((bf16[256,8,128]{2,1,0:T(8,128)(2,1)S(1)}, bf16[256,8,128]{2,1,0:T(8,128)(2,1)}, u32[]{:S(2)}) %copy-start) | copy-done | bytes 524312
  1.7 0.0 copy-start.1
  1.7 1.0 %copy-done.1 = bf16[256,8,128]{2,1,0:T(8,128)(2,1)S(1)} copy-done((bf16[256,8,128]{2,1,0:T(8,128)(2,1)S(1)}, bf16[256,8,128]{2,1,0:T(8,128)(2,1)}, u32[]{:S(2)}) %copy-start.1) | copy-done | bytes 524312
  2.7 0.0 copy-start.2
  2.7 0.8 %copy-done.2 = bf16[256,1,128]{2,0,1:T(8,128)(2,1)S(1)} copy-done((bf16[256,1,128]{2,0,1:T(8,128)(2,1)S(1)}, bf16[256,1,128]{2,0,1:T(8,128)(2,1)}, u32[]{:S(2)}) %copy-start.2) | copy-done | bytes 65560
  3.6 0.0 copy-start.3
  3.6 0.8 %copy-done.3 = bf16[256,1,128]{2,0,1:T(8,128)(2,1)S(1)} copy-done((bf16[256,1,128]{2,0,1:T(8,128)(2,1)S(1)}, bf16[256,1,128]{2,0,1:T(8,128)(2,1)}, u32[]{:S(2)}) %copy-start.3) | copy-done | bytes 65560
  4.4 0.0 copy-start.4
  4.4 0.7 copy-done.4
  5.1 33.6 %shard_map.93 = (bf16[2,16,128,128]{3,2,1,0:T(8,128)(2,1)S(1)}, bf16[16,256,128]{2,1,0:T(8,128)(2,1)S(1)}, bf16[16,256,128]{2,1,0:T(8,128)(2,1)S(1)}, bf16[256,4096]{1,0:T(8,128)(2,1)S(1)}) custom-call(s32[16,16]{1,0:T(8,128)S(1)} %copy-done.4, bf16[16,128,128]{2,1,0:T(8,128)(2,1)S(1)} %bitcast.16, bf16[16,128,128]{2,1,0:T(8,128)(2,1)S(1)} %bitcast.17, ...), custom_call_target="tpu_custom_call" | custom-call | tf_op jit(solution)/shard_map/pallas_call | solution.py:197
  38.7 0.0 copy-start.5
  38.7 0.7 copy-done.5
  39.4 0.0 copy-start.6
  39.4 0.7 copy-done.6
  40.0 14.3 %shard_map.94 = (bf16[16,128,128]{2,1,0:T(8,128)(2,1)}, bf16[16,128,128]{2,1,0:T(8,128)(2,1)}, bf16[16,16,16,128]{3,2,1,0:T(8,128)(2,1)S(1)}, bf16[16,16,16,128]{3,2,1,0:T(8,128)(2,1)S(1)}) custom-call(s32[8]{0:T(128)S(1)} %copy-done.6, s32[16,16]{1,0:T(8,128)S(1)} %copy-done.5, bf16[2,16,128,128]{3,2,1,0:T(8,128)(2,1)S(1)} %get-tuple-element.14.qg_ref, ...), custom_call_target="tpu_custom_call" | custom-call | tf_op jit(solution)/shard_map/pallas_call | solution.py:523
  54.3 21.9 %shard_map.95 = (bf16[256,128]{1,0:T(8,128)(2,1)S(1)}, bf16[256,128]{1,0:T(8,128)(2,1)S(1)}) custom-call(bf16[16,256,128]{2,1,0:T(8,128)(2,1)S(1)} %bitcast.12, bf16[16,256,128]{2,1,0:T(8,128)(2,1)S(1)} %bitcast.13), custom_call_target="tpu_custom_call" | custom-call | tf_op jit(solution)/shard_map/pallas_call | solution.py:336
  76.3 0.6 copy.12
  76.9 0.6 copy.13
Async XLA Ops:
  0.6 1.0 %copy-start = (bf16[256,8,128]{2,1,0:T(8,128)(2,1)S(1)}, bf16[256,8,128]{2,1,0:T(8,128)(2,1)}, u32[]{:S(2)}) copy-start(bf16[256,8,128]{2,1,0:T(8,128)(2,1)} %param.6) | copy-start | bytes 1572868
  1.7 1.0 %copy-start.1 = (bf16[256,8,128]{2,1,0:T(8,128)(2,1)S(1)}, bf16[256,8,128]{2,1,0:T(8,128)(2,1)}, u32[]{:S(2)}) copy-start(bf16[256,8,128]{2,1,0:T(8,128)(2,1)} %param.9) | copy-start | bytes 1572868
  2.7 0.8 %copy-start.2 = (bf16[256,1,128]{2,0,1:T(8,128)(2,1)S(1)}, bf16[256,1,128]{2,0,1:T(8,128)(2,1)}, u32[]{:S(2)}) copy-start(bf16[256,1,128]{2,0,1:T(8,128)(2,1)} %param.7) | copy-start | bytes 196612
  3.6 0.8 %copy-start.3 = (bf16[256,1,128]{2,0,1:T(8,128)(2,1)S(1)}, bf16[256,1,128]{2,0,1:T(8,128)(2,1)}, u32[]{:S(2)}) copy-start(bf16[256,1,128]{2,0,1:T(8,128)(2,1)} %param.8) | copy-start | bytes 196612
  4.4 0.7 copy-start.4
  38.7 0.7 copy-start.5
  39.4 0.7 copy-start.6

commit v5 on v4

--- a/solution.py
+++ b/solution.py
@@ -130,6 +130,13 @@
     loads[2].wait()
     loads[3].wait()
 
+    def turn(spread, a, b):
+        row = 0 if spread.first_is_y else width
+        block = spread.block(a, b)
+        for h in range(k_out.shape[1] // 128):
+            at = pl.ds(pl.multiple_of(block * k_out.shape[1] + h * 128, 128), 128)
+            kvt[row:row + width, at] = spread.blocks[block, h * 128:(h + 1) * 128].T
+
     def slot_for(target):
         slot = jnp.int32(0)
         for s in range(SIDE * SIDE):
@@ -151,11 +158,16 @@
             spread.got(1, 0, kind)
             spread.onward(1, 0, kind)
             spread.second(-1 if kind == 0 else 1)
+    for spread in spreads:
+        for a in (0, -1, 1):
+            turn(spread, a, 0)
     reassign(far[5:10])
     for spread in spreads:
         spread.got(1, 0, 2)
         spread.got(1, 0, 3)
         spread.second(2)
+    for spread in spreads:
+        turn(spread, 2, 0)
     for kind in (0, 1):
         for spread in spreads:
             spread.got(2, 0, kind)
@@ -169,17 +181,16 @@
             for spread in spreads:
                 spread.got(2, a, kind)
                 spread.onward(2, a, kind)
+    for spread in spreads:
+        for a in (0, -1, 1, 2):
+            for b in (-1, 1):
+                turn(spread, a, b)
     for a in (0, -1, 1, 2):
         for kind in (2, 3):
             for spread in spreads:
                 spread.got(2, a, kind)
-
-    @pl.loop(0, SIDE * SIDE)
-    def _(b):
-        for h in range(k_out.shape[1] // 128):
-            at = pl.ds(pl.multiple_of(b * k_out.shape[1] + h * 128, 128), 128)
-            kvt[0:width, at] = k_out[b, h * 128:(h + 1) * 128].T
-            kvt[width:2 * width, at] = v_out[b, h * 128:(h + 1) * 128].T
+        for spread in spreads:
+            turn(spread, a, 2)
 
     for n in far:
         dz, dy = OFFSETS[n]
@@ -221,12 +232,11 @@
     PLUS, MINUS = (2, 0), (1, 3)
 
     def __init__(self, first_is_y, blocks, out, copies, base, passing, joined, left, right,
-                 sums, own_sum, passing2, joined2, left2, right2):
+                 sums, own_sum, far2, left2, right2):
         self.first_is_y, self.blocks, self.out, self.copies, self.base = first_is_y, blocks, out, copies, base
         self.passing, self.joined, self.left, self.right = passing, joined, left, right
         self.sums, self.own_sum = sums, own_sum
-        self.passing2, self.joined2, self.left2, self.right2 = passing2, joined2, left2, right2
-        self.half = out.shape[0] // 2
+        self.far2, self.left2, self.right2 = far2, left2, right2
 
     def device(self, a, b):
         return device_at(b, a) if self.first_is_y else device_at(a, b)
@@ -264,51 +274,27 @@
         else:
             self.sums[b] = total.astype(jnp.bfloat16)
 
-    def rows(self, half):
-        return pl.ds(half * self.half, self.half)
-
     def begin2(self, b):
-        if b == 2:
-            for half in (0, 1):
-                self.copies.send(self.base + 12 + half, self.sums.at[2, self.rows(half)],
-                                 self.passing2.at[half], self.device(0, 1 - 2 * half))
-        elif b == 1:
-            self.copies.send(self.base + 14, self.sums.at[1, self.rows(1)],
-                             self.left2.at[self.rows(1)], self.device(0, 1))
-        else:
-            self.copies.send(self.base + 15, self.sums.at[3, self.rows(0)],
-                             self.right2.at[self.rows(0)], self.device(0, -1))
-
-    def join2(self, half):
-        self.copies.arrived(self.base + 12 + half, self.passing2.at[half])
-        b = 1 if half == 0 else 3
-        mine = self.sums[b, self.rows(half)].astype(jnp.float32)
-        self.joined2[half] = (mine + self.passing2[half].astype(jnp.float32)).astype(jnp.bfloat16)
-        if half == 0:
-            self.copies.send(self.base + 16, self.joined2.at[0], self.left2.at[self.rows(0)],
-                             self.device(0, 1))
-        else:
-            self.copies.send(self.base + 17, self.joined2.at[1], self.right2.at[self.rows(1)],
-                             self.device(0, -1))
+        land = {1: self.left2, 2: self.far2, 3: self.right2}[b]
+        self.copies.send(self.base + 11 + b, self.sums.at[b], land, self.device(0, b))
 
     def end(self):
-        self.copies.arrived(self.base + 14, self.left2.at[self.rows(1)])
-        self.copies.arrived(self.base + 15, self.right2.at[self.rows(0)])
-        self.copies.arrived(self.base + 16, self.left2.at[self.rows(0)])
-        self.copies.arrived(self.base + 17, self.right2.at[self.rows(1)])
-        total = self.own_sum[...] + self.left2[...].astype(jnp.float32) + self.right2[...].astype(jnp.float32)
+        total = self.own_sum[...]
+        for b, land in ((1, self.left2), (2, self.far2), (3, self.right2)):
+            self.copies.arrived(self.base + 11 + b, land)
+            total = total + land[...].astype(jnp.float32)
         self.out[...] = total.astype(jnp.bfloat16)
 
 
 def collect_kernel(dk_ref, dv_ref, dk_out, dv_out, passing, joined, left, right, sums, own_sum,
-                   passing2, joined2, left2, right2, send_sems, recv_sems):
+                   far2, left2, right2, send_sems, recv_sems):
     copies = Copies(send_sems, recv_sems)
     k_sum, v_sum = [
-        Collect(i == 0, blocks, out, copies, 18 * i, passing.at[i], joined.at[i], left.at[i], right.at[i],
-                sums.at[i], own_sum.at[i], passing2.at[i], joined2.at[i], left2.at[i], right2.at[i])
+        Collect(i == 0, blocks, out, copies, 15 * i, passing.at[i], joined.at[i], left.at[i], right.at[i],
+                sums.at[i], own_sum.at[i], far2.at[i], left2.at[i], right2.at[i])
         for i, (blocks, out) in enumerate(((dk_ref, dk_out), (dv_ref, dv_out)))]
     both = (k_sum, v_sum)
-    greet([(1, 0), (3, 0), (0, 1), (0, 3)])
+    greet([(1, 0), (2, 0), (3, 0), (0, 1), (0, 2), (0, 3)])
     for one in both:
         one.begin()
     for b in (2, 1, 0, 3):
@@ -318,9 +304,6 @@
         for one in both:
             one.total(b)
             one.begin2(b)
-    for half in (0, 1):
-        for one in both:
-            one.join2(half)
     for one in both:
         one.total(0)
     for one in both:
@@ -341,10 +324,9 @@
         scratch_shapes=[
             pltpu.VMEM(full, bf16), pltpu.VMEM(full, bf16), pltpu.VMEM(full, bf16), pltpu.VMEM(full, bf16),
             pltpu.VMEM(full, bf16), pltpu.VMEM((2, local, width), jnp.float32),
-            pltpu.VMEM((2, 2, local // 2, width), bf16), pltpu.VMEM((2, 2, local // 2, width), bf16),
-            pltpu.VMEM((2, local, width), bf16), pltpu.VMEM((2, local, width), bf16),
-            pltpu.SemaphoreType.DMA((36,)),
-            pltpu.SemaphoreType.DMA((36,)),
+            pltpu.VMEM((2, local, width), bf16), pltpu.VMEM((2, local, width), bf16), pltpu.VMEM((2, local, width), bf16),
+            pltpu.SemaphoreType.DMA((30,)),
+            pltpu.SemaphoreType.DMA((30,)),
         ],
         compiler_params=pltpu.CompilerParams(
             collective_id=1, has_side_effects=True, vmem_limit_bytes=24 << 20),
@@ -551,8 +533,10 @@
     local, heads, width = query.shape
     shards = SIDE * SIDE
     rows = local // shards * heads
-    qg, k, v, kvt = exchange(block_owner, query.reshape(shards, rows, width),
-                             output_gradient.reshape(shards, rows, width), keys[:, 0], values[:, 0])
+    loaded = (query.reshape(shards, rows, width), output_gradient.reshape(shards, rows, width),
+              keys[:, 0], values[:, 0])
+    loaded = [pltpu.with_memory_space_constraint(one, pltpu.HBM) for one in loaded]
+    qg, k, v, kvt = exchange(block_owner, *loaded)
     out, dq, dk, dv = attention(qg, k, v, kvt, doc_lengths, block_owner)
     dk, dv = collect(dk, dv)
     return (

time: 77.9 us -> 70.7 us (0.908)
  local copies, waits for them, and re-layouts: 7.06 us -> 3.3 us
  Pallas kernels: 69.8 us -> 66.5 us
    pallas_call x1, Pallas kernels: 21.9 us -> 17.7 us  [collect(): pl.pallas_call(collect_kernel, out_shape=(jax.ShapeDtypeStruct((local, wi...]
    unnamed x16 -> x8, local copies, waits for them, and re-layouts: 7.06 us -> 3.3 us
    pallas_call x1, Pallas kernels: 14.3 us -> 16.8 us  [attention(): pl.pallas_call(functools.partial(attention_kernel, width ** (-0.5), me),...]
    pallas_call x1, Pallas kernels: 33.6 us -> 32 us  [exchange(): pl.pallas_call(exchange_kernel, out_shape=(jax.ShapeDtypeStruct((2, shard...]
where the time goes in v5:
time: 70.7 us; the launch traced here: 70.4 us
  Pallas kernels  66.5 us (94%)
  local copies, waits for them, and re-layouts  3.3 us (5%)
    pallas_call x1, Pallas kernels, exchange(): pl.pallas_call(exchange_kernel, out_shape=(jax.ShapeDtypeStruct((2, shard...  32 us
    pallas_call x1, Pallas kernels, collect(): pl.pallas_call(collect_kernel, out_shape=(jax.ShapeDtypeStruct((local, wi...  17.7 us
    pallas_call x1, Pallas kernels, attention(): pl.pallas_call(functools.partial(attention_kernel, width ** (-0.5), me),...  16.8 us
    unnamed x8, local copies, waits for them, and re-layouts  3.3 us

profile of v5, /device:TPU:0, one launch (start us, length us, event | category | flops | bytes accessed | tf_op | source)
XLA Modules:
  0.0 70.4 jit_solution(834594089502430365)
XLA Ops:
  0.6 0.0 copy-start
  0.6 0.7 copy-done
  1.3 32.0 %shard_map.93 = (bf16[2,16,128,128]{3,2,1,0:T(8,128)(2,1)S(1)}, bf16[16,256,128]{2,1,0:T(8,128)(2,1)S(1)}, bf16[16,256,128]{2,1,0:T(8,128)(2,1)S(1)}, bf16[256,4096]{1,0:T(8,128)(2,1)S(1)}) custom-call(s32[16,16]{1,0:T(8,128)S(1)} %copy-done, bf16[16,128,128]{2,1,0:T(8,128)(2,1)} %bitcast.18, bf16[16,128,128]{2,1,0:T(8,128)(2,1)} %bitcast.19, ...), custom_call_target="tpu_custom_call" | custom-call | tf_op jit(solution)/shard_map/pallas_call | solution.py:208
  33.3 0.0 copy-start.1
  33.3 0.7 copy-done.1
  34.0 0.0 copy-start.2
  34.0 0.7 copy-done.2
  34.6 16.8 %shard_map.94 = (bf16[16,128,128]{2,1,0:T(8,128)(2,1)}, bf16[16,128,128]{2,1,0:T(8,128)(2,1)}, bf16[16,16,16,128]{3,2,1,0:T(8,128)(2,1)S(1)}, bf16[16,16,16,128]{3,2,1,0:T(8,128)(2,1)S(1)}) custom-call(s32[8]{0:T(128)S(1)} %copy-done.2, s32[16,16]{1,0:T(8,128)S(1)} %copy-done.1, bf16[2,16,128,128]{3,2,1,0:T(8,128)(2,1)S(1)} %get-tuple-element.14.qg_ref, ...), custom_call_target="tpu_custom_call" | custom-call | tf_op jit(solution)/shard_map/pallas_call | solution.py:505
  51.4 17.7 %shard_map.95 = (bf16[256,128]{1,0:T(8,128)(2,1)S(1)}, bf16[256,128]{1,0:T(8,128)(2,1)S(1)}) custom-call(bf16[16,256,128]{2,1,0:T(8,128)(2,1)S(1)} %bitcast.12, bf16[16,256,128]{2,1,0:T(8,128)(2,1)S(1)} %bitcast.13), custom_call_target="tpu_custom_call" | custom-call | tf_op jit(solution)/shard_map/pallas_call | solution.py:319
  69.2 0.6 copy.12
  69.8 0.6 copy.13
Async XLA Ops:
  0.6 0.7 copy-start
  33.3 0.7 copy-start.1
  34.0 0.7 copy-start.2

commit v6 on v5

--- a/solution.py
+++ b/solution.py
@@ -112,12 +112,12 @@
             self.send(2, a, kind, part, part)
 
 
-def exchange_kernel(owners, q_hbm, g_hbm, k_hbm, v_hbm, qg_out, k_out, v_out, kvt,
-                    q_in, g_in, staging, load_sems, send_sems, recv_sems):
+def exchange_kernel(owners_hbm, q_hbm, g_hbm, k_hbm, v_hbm, qg_out, k_out, v_out, kvt,
+                    owners, q_in, g_in, staging, load_sems, send_sems, recv_sems):
     me = lax.axis_index(MESH_AXIS)
     width = k_out.shape[2]
     loads = [pltpu.make_async_copy(src, dst, load_sems.at[n]) for n, (src, dst) in enumerate((
-        (k_hbm, k_out.at[me]), (v_hbm, v_out.at[me]), (q_hbm, q_in), (g_hbm, g_in)))]
+        (k_hbm, k_out.at[me]), (v_hbm, v_out.at[me]), (q_hbm, q_in), (g_hbm, g_in), (owners_hbm, owners)))]
     for load in loads:
         load.start()
     copies = Copies(send_sems, recv_sems)
@@ -129,6 +129,7 @@
         spread.start()
     loads[2].wait()
     loads[3].wait()
+    loads[4].wait()
 
     def turn(spread, a, b):
         row = 0 if spread.first_is_y else width
@@ -201,7 +202,6 @@
 def exchange(owners, q, g, k, v):
     shards, rows, width = q.shape
     local = k.shape[0]
-    smem = pl.BlockSpec(memory_space=pltpu.SMEM)
     vmem = pl.BlockSpec(memory_space=pltpu.VMEM)
     hbm = pl.BlockSpec(memory_space=pltpu.HBM)
     bf16 = jnp.bfloat16
@@ -213,13 +213,14 @@
             jax.ShapeDtypeStruct((shards, local, width), bf16),
             jax.ShapeDtypeStruct((2 * width, shards * local), bf16),
         ),
-        in_specs=[smem, hbm, hbm, hbm, hbm],
+        in_specs=[hbm] * 5,
         out_specs=(vmem, vmem, vmem, vmem),
         scratch_shapes=[
+            pltpu.SMEM(owners.shape, jnp.int32),
             pltpu.VMEM((shards, rows, width), bf16),
             pltpu.VMEM((shards, rows, width), bf16),
             pltpu.VMEM((shards - 1, 2, rows, width), bf16),
-            pltpu.SemaphoreType.DMA((4,)),
+            pltpu.SemaphoreType.DMA((5,)),
             pltpu.SemaphoreType.DMA((55,)),
             pltpu.SemaphoreType.DMA((55,)),
         ],
@@ -337,14 +338,14 @@
 CHUNK = 256
 
 
-def attention_kernel(scale, me, lengths, owners, qg_ref, k_ref, v_ref, kvt,
+def attention_kernel(scale, me, lengths_hbm, owners_hbm, qg_ref, k_ref, v_ref, kvt,
                      out_hbm, dq_hbm, dk_ref, dv_ref,
-                     dk_acc, dv_acc, out_buf, dq_buf, sems, *lanes):
+                     lengths, owners, load_sems, dk_acc, dv_acc, out_buf, dq_buf, sems, *lanes):
     if me is None:
         me = lax.axis_index("ctx")
     _, shards, rows, width = qg_ref.shape
     keys = k_ref.shape[0]
-    ndocs = lengths.shape[0]
+    ndocs = lengths_hbm.shape[0]
     shard_rows = keys // shards
     block = shard_rows // shards
     heads = rows // block
@@ -353,8 +354,14 @@
     together = len(lanes) // 3
     lanes = [lanes[3 * n:3 * n + 3] for n in range(together)]
 
+    loads = [pltpu.make_async_copy(src, dst, load_sems.at[n])
+             for n, (src, dst) in enumerate(((lengths_hbm, lengths), (owners_hbm, owners)))]
+    for load in loads:
+        load.start()
     dk_acc[...] = jnp.zeros_like(dk_acc)
     dv_acc[...] = jnp.zeros_like(dv_acc)
+    for load in loads:
+        load.wait()
     token = lax.broadcasted_iota(jnp.int32, (1, rows), 1) // heads
     key_index = lax.broadcasted_iota(jnp.int32, (CHUNK, rows), 0)
 
@@ -498,7 +505,6 @@
     local = k.shape[1]
     keys = shards * local
     block = keys // shards // shards
-    smem = pl.BlockSpec(memory_space=pltpu.SMEM)
     vmem = pl.BlockSpec(memory_space=pltpu.VMEM)
     hbm = pl.BlockSpec(memory_space=pltpu.HBM)
     f32, bf16 = jnp.float32, jnp.bfloat16
@@ -510,9 +516,12 @@
             jax.ShapeDtypeStruct((shards, shards, block, width), bf16),
             jax.ShapeDtypeStruct((shards, shards, block, width), bf16),
         ),
-        in_specs=[smem, smem, vmem, vmem, vmem, vmem],
+        in_specs=[hbm, hbm, vmem, vmem, vmem, vmem],
         out_specs=(hbm, hbm, vmem, vmem),
         scratch_shapes=[
+            pltpu.SMEM(lengths.shape, jnp.int32),
+            pltpu.SMEM(owners.shape, jnp.int32),
+            pltpu.SemaphoreType.DMA((2,)),
             pltpu.VMEM((keys, width), f32),
             pltpu.VMEM((keys, width), f32),
             pltpu.VMEM((shards, rows, width), bf16),
@@ -536,8 +545,9 @@
     loaded = (query.reshape(shards, rows, width), output_gradient.reshape(shards, rows, width),
               keys[:, 0], values[:, 0])
     loaded = [pltpu.with_memory_space_constraint(one, pltpu.HBM) for one in loaded]
-    qg, k, v, kvt = exchange(block_owner, *loaded)
-    out, dq, dk, dv = attention(qg, k, v, kvt, doc_lengths, block_owner)
+    lengths, owners = [pltpu.with_memory_space_constraint(one, pltpu.HBM) for one in (doc_lengths, block_owner)]
+    qg, k, v, kvt = exchange(owners, *loaded)
+    out, dq, dk, dv = attention(qg, k, v, kvt, lengths, owners)
     dk, dv = collect(dk, dv)
     return (
         out.reshape(local, heads, width),

time: 70.7 us -> 68.8 us (0.973)
  local copies, waits for them, and re-layouts: 3.3 us -> 1.26 us
    unnamed x8 -> x2, local copies, waits for them, and re-layouts: 3.3 us -> 1.26 us
    pallas_call x1, Pallas kernels: 17.7 us -> 18.5 us  [collect(): pl.pallas_call(collect_kernel, out_shape=(jax.ShapeDtypeStruct((local, wi...]
where the time goes in v6:
time: 68.8 us; the launch traced here: 68.6 us
  Pallas kernels  66.7 us (97%)
  local copies, waits for them, and re-layouts  1.26 us (2%)
    pallas_call x1, Pallas kernels, exchange(): pl.pallas_call(exchange_kernel, out_shape=(jax.ShapeDtypeStruct((2, shard...  31.4 us
    pallas_call x1, Pallas kernels, collect(): pl.pallas_call(collect_kernel, out_shape=(jax.ShapeDtypeStruct((local, wi...  18.5 us
    pallas_call x1, Pallas kernels, attention(): pl.pallas_call(functools.partial(attention_kernel, width ** (-0.5), me),...  16.9 us

profile of v6, /device:TPU:0, one launch (start us, length us, event | category | flops | bytes accessed | tf_op | source)
XLA Modules:
  0.0 68.6 jit_solution(10855184350525004799)
XLA Ops:
  0.6 31.4 %shard_map.93 = (bf16[2,16,128,128]{3,2,1,0:T(8,128)(2,1)S(1)}, bf16[16,256,128]{2,1,0:T(8,128)(2,1)S(1)}, bf16[16,256,128]{2,1,0:T(8,128)(2,1)S(1)}, bf16[256,4096]{1,0:T(8,128)(2,1)S(1)}) custom-call(s32[16,16]{1,0:T(8,128)} %owners_hbm.3, bf16[16,128,128]{2,1,0:T(8,128)(2,1)} %bitcast.18, bf16[16,128,128]{2,1,0:T(8,128)(2,1)} %bitcast.19, ...), custom_call_target="tpu_custom_call" | custom-call | tf_op jit(solution)/shard_map/pallas_call | solution.py:208
  32.0 16.9 %shard_map.94 = (bf16[16,128,128]{2,1,0:T(8,128)(2,1)}, bf16[16,128,128]{2,1,0:T(8,128)(2,1)}, bf16[16,16,16,128]{3,2,1,0:T(8,128)(2,1)S(1)}, bf16[16,16,16,128]{3,2,1,0:T(8,128)(2,1)S(1)}) custom-call(s32[8]{0:T(128)} %lengths_hbm.1, s32[16,16]{1,0:T(8,128)} %owners_hbm.3, bf16[2,16,128,128]{3,2,1,0:T(8,128)(2,1)S(1)} %get-tuple-element.14.qg_ref, ...), custom_call_target="tpu_custom_call" | custom-call | tf_op jit(solution)/shard_map/pallas_call | solution.py:511
  48.9 18.5 %shard_map.95 = (bf16[256,128]{1,0:T(8,128)(2,1)S(1)}, bf16[256,128]{1,0:T(8,128)(2,1)S(1)}) custom-call(bf16[16,256,128]{2,1,0:T(8,128)(2,1)S(1)} %bitcast.12, bf16[16,256,128]{2,1,0:T(8,128)(2,1)S(1)} %bitcast.13), custom_call_target="tpu_custom_call" | custom-call | tf_op jit(solution)/shard_map/pallas_call | solution.py:320
  67.4 0.6 copy.12
  68.0 0.6 copy.13

commit v7 on v6

--- a/solution.py
+++ b/solution.py
@@ -121,15 +121,12 @@
     for load in loads:
         load.start()
     copies = Copies(send_sems, recv_sems)
-    spreads = (Spread(True, k_out.at[me], k_out, copies, 0), Spread(False, v_out.at[me], v_out, copies, 20))
+    spreads = (Spread(True, k_hbm, k_out, copies, 0), Spread(False, v_hbm, v_out, copies, 20))
     greet(OFFSETS)
-    loads[0].wait()
-    loads[1].wait()
     for spread in spreads:
         spread.start()
-    loads[2].wait()
-    loads[3].wait()
-    loads[4].wait()
+    for load in loads:
+        load.wait()
 
     def turn(spread, a, b):
         row = 0 if spread.first_is_y else width
@@ -152,28 +149,23 @@
             staging[n, 1] = g_in[slot]
             copies.send(40 + n, staging.at[n], qg_out.at[:, me], target)
 
-    far = sorted(range(15), key=lambda n: -sum(min(d, SIDE - d) for d in OFFSETS[n]))
-    reassign(far[:5])
+    far = sorted(range(15), key=lambda n: sum(min(d, SIDE - d) for d in OFFSETS[n]))
+    reassign(far[:4])
     for kind in (0, 1):
         for spread in spreads:
             spread.got(1, 0, kind)
             spread.onward(1, 0, kind)
             spread.second(-1 if kind == 0 else 1)
-    for spread in spreads:
-        for a in (0, -1, 1):
-            turn(spread, a, 0)
-    reassign(far[5:10])
+    reassign(far[4:9])
     for spread in spreads:
         spread.got(1, 0, 2)
         spread.got(1, 0, 3)
         spread.second(2)
-    for spread in spreads:
-        turn(spread, 2, 0)
     for kind in (0, 1):
         for spread in spreads:
             spread.got(2, 0, kind)
             spread.onward(2, 0, kind)
-    reassign(far[10:])
+    reassign(far[9:])
     slot = slot_for(me)
     qg_out[0, me] = q_in[slot]
     qg_out[1, me] = g_in[slot]
@@ -184,7 +176,7 @@
                 spread.onward(2, a, kind)
     for spread in spreads:
         for a in (0, -1, 1, 2):
-            for b in (-1, 1):
+            for b in (0, -1, 1):
                 turn(spread, a, b)
     for a in (0, -1, 1, 2):
         for kind in (2, 3):

time: 68.8 us -> 66.6 us (0.968)
  Pallas kernels: 66.7 us -> 64.8 us
    pallas_call x1, Pallas kernels: 18.5 us -> 16.2 us  [collect(): pl.pallas_call(collect_kernel, out_shape=(jax.ShapeDtypeStruct((local, wi...]
where the time goes in v7:
time: 66.6 us; the launch traced here: 66.7 us
  Pallas kernels  64.8 us (97%)
  local copies, waits for them, and re-layouts  1.26 us (2%)
    pallas_call x1, Pallas kernels, exchange(): pl.pallas_call(exchange_kernel, out_shape=(jax.ShapeDtypeStruct((2, shard...  31.9 us
    pallas_call x1, Pallas kernels, attention(): pl.pallas_call(functools.partial(attention_kernel, width ** (-0.5), me),...  16.7 us
    pallas_call x1, Pallas kernels, collect(): pl.pallas_call(collect_kernel, out_shape=(jax.ShapeDtypeStruct((local, wi...  16.2 us

profile of v7, /device:TPU:0, one launch (start us, length us, event | category | flops | bytes accessed | tf_op | source)
XLA Modules:
  0.0 66.7 jit_solution(3129379426730152932)
XLA Ops:
  0.6 31.9 %shard_map.93 = (bf16[2,16,128,128]{3,2,1,0:T(8,128)(2,1)S(1)}, bf16[16,256,128]{2,1,0:T(8,128)(2,1)S(1)}, bf16[16,256,128]{2,1,0:T(8,128)(2,1)S(1)}, bf16[256,4096]{1,0:T(8,128)(2,1)S(1)}) custom-call(s32[16,16]{1,0:T(8,128)} %owners_hbm.3, bf16[16,128,128]{2,1,0:T(8,128)(2,1)} %bitcast.18, bf16[16,128,128]{2,1,0:T(8,128)(2,1)} %bitcast.19, ...), custom_call_target="tpu_custom_call" | custom-call | tf_op jit(solution)/shard_map/pallas_call | solution.py:200
  32.5 16.7 %shard_map.94 = (bf16[16,128,128]{2,1,0:T(8,128)(2,1)}, bf16[16,128,128]{2,1,0:T(8,128)(2,1)}, bf16[16,16,16,128]{3,2,1,0:T(8,128)(2,1)S(1)}, bf16[16,16,16,128]{3,2,1,0:T(8,128)(2,1)S(1)}) custom-call(s32[8]{0:T(128)} %lengths_hbm.1, s32[16,16]{1,0:T(8,128)} %owners_hbm.3, bf16[2,16,128,128]{3,2,1,0:T(8,128)(2,1)S(1)} %get-tuple-element.14.qg_ref, ...), custom_call_target="tpu_custom_call" | custom-call | tf_op jit(solution)/shard_map/pallas_call | solution.py:503
  49.2 16.2 %shard_map.95 = (bf16[256,128]{1,0:T(8,128)(2,1)S(1)}, bf16[256,128]{1,0:T(8,128)(2,1)S(1)}) custom-call(bf16[16,256,128]{2,1,0:T(8,128)(2,1)S(1)} %bitcast.12, bf16[16,256,128]{2,1,0:T(8,128)(2,1)S(1)} %bitcast.13), custom_call_target="tpu_custom_call" | custom-call | tf_op jit(solution)/shard_map/pallas_call | solution.py:312
  65.4 0.6 copy.12
  66.0 0.6 copy.13

commit v8 on v7

--- a/solution.py
+++ b/solution.py
@@ -396,7 +396,7 @@
             span = pl.ds(self.at + c * CHUNK, CHUNK)
             raw = dot(k_ref[span, :], self.q[...], NT)
             self.d_buf[here, :] = dot(v_ref[span, :], self.g[...], NT)
-            allowed = (key_index >= self.lower - c * CHUNK) & (key_index <= self.upper - c * CHUNK)
+            allowed = (key_index - (self.lower - c * CHUNK)).astype(jnp.uint32) <= (self.upper - self.lower).astype(jnp.uint32)
             x = jnp.where(allowed, raw, NEG)
             self.s_buf[here, :] = x
             self.peak = jnp.maximum(self.peak, folded(x, jnp.max))

time: 66.6 us -> 67.3 us (1.011)
    pallas_call x1, Pallas kernels: 16.2 us -> 17.5 us  [collect(): pl.pallas_call(collect_kernel, out_shape=(jax.ShapeDtypeStruct((local, wi...]
    pallas_call x1, Pallas kernels: 16.7 us -> 15.6 us  [attention(): pl.pallas_call(functools.partial(attention_kernel, width ** (-0.5), me),...]
where the time goes in v8:
time: 67.3 us; the launch traced here: 66.9 us
  Pallas kernels  65 us (97%)
  local copies, waits for them, and re-layouts  1.26 us (2%)
    pallas_call x1, Pallas kernels, exchange(): pl.pallas_call(exchange_kernel, out_shape=(jax.ShapeDtypeStruct((2, shard...  31.9 us
    pallas_call x1, Pallas kernels, collect(): pl.pallas_call(collect_kernel, out_shape=(jax.ShapeDtypeStruct((local, wi...  17.5 us
    pallas_call x1, Pallas kernels, attention(): pl.pallas_call(functools.partial(attention_kernel, width ** (-0.5), me),...  15.6 us

profile of v8, /device:TPU:0, one launch (start us, length us, event | category | flops | bytes accessed | tf_op | source)
XLA Modules:
  0.0 66.9 jit_solution(17216738178145571710)
XLA Ops:
  0.6 31.9 %shard_map.93 = (bf16[2,16,128,128]{3,2,1,0:T(8,128)(2,1)S(1)}, bf16[16,256,128]{2,1,0:T(8,128)(2,1)S(1)}, bf16[16,256,128]{2,1,0:T(8,128)(2,1)S(1)}, bf16[256,4096]{1,0:T(8,128)(2,1)S(1)}) custom-call(s32[16,16]{1,0:T(8,128)} %owners_hbm.3, bf16[16,128,128]{2,1,0:T(8,128)(2,1)} %bitcast.18, bf16[16,128,128]{2,1,0:T(8,128)(2,1)} %bitcast.19, ...), custom_call_target="tpu_custom_call" | custom-call | tf_op jit(solution)/shard_map/pallas_call | solution.py:200
  32.5 15.6 %shard_map.94 = (bf16[16,128,128]{2,1,0:T(8,128)(2,1)}, bf16[16,128,128]{2,1,0:T(8,128)(2,1)}, bf16[16,16,16,128]{3,2,1,0:T(8,128)(2,1)S(1)}, bf16[16,16,16,128]{3,2,1,0:T(8,128)(2,1)S(1)}) custom-call(s32[8]{0:T(128)} %lengths_hbm.1, s32[16,16]{1,0:T(8,128)} %owners_hbm.3, bf16[2,16,128,128]{3,2,1,0:T(8,128)(2,1)S(1)} %get-tuple-element.14.qg_ref, ...), custom_call_target="tpu_custom_call" | custom-call | tf_op jit(solution)/shard_map/pallas_call | solution.py:503
  48.1 17.5 %shard_map.95 = (bf16[256,128]{1,0:T(8,128)(2,1)S(1)}, bf16[256,128]{1,0:T(8,128)(2,1)S(1)}) custom-call(bf16[16,256,128]{2,1,0:T(8,128)(2,1)S(1)} %bitcast.12, bf16[16,256,128]{2,1,0:T(8,128)(2,1)S(1)} %bitcast.13), custom_call_target="tpu_custom_call" | custom-call | tf_op jit(solution)/shard_map/pallas_call | solution.py:312
  65.7 0.6 copy.12
  66.3 0.6 copy.13
